TPU v7x, 256 devices: a whole 4x4x8 slice. The times are simulated.
256 devices in a mesh: comp: 2 (over z_lo), tgt: 16 (over y, x), src: 8 (over z_hi, core).
Axes of the slice: x: 4, y: 4, z: 8 (z_hi: 4, z_lo: 2; z = z_hi * 2 + z_lo), core: 2. Of those that a mesh axis runs over, the one named last changes fastest.
Arguments:
- field: bfloat16 [3, 32, 65536], P(None, None, ('tgt', 'src')), may hold values from -6 to 6
- dest_group: int32 [32768, 1], P(('comp', 'tgt', 'src')), may hold values from 0 to 15; in each aligned block of 128 rows (0 to 127, 128 to 255, ...) at most 16 rows name the same one
- src_local: int32 [32768], P(('comp', 'tgt', 'src')), may hold values from 0 to 1
- ranks: int32 [32768], P(('comp', 'tgt', 'src')), may hold values from 8 to 64
- mixing: float32 [32768, 3, 3], P(('comp', 'tgt', 'src')), may hold values from -5 to 5
- v_factor: bfloat16 [32768, 64, 256], P(('comp', 'tgt', 'src')), may hold values from -0.375 to 0.375
- u_factor: bfloat16 [65536, 64, 256], P(('comp', 'tgt', 'src')), may hold values from -0.0625 to 0.0625
- slot_cluster: int32 [65536], P(('comp', 'tgt', 'src')), may hold values from 0 to 15
- near_src: int32 [1024], P(('comp', 'tgt', 'src')), may hold values from 0 to 1
- near_tgt: int32 [1024], P(('comp', 'tgt', 'src')), may hold values from 0 to 15
- near_mixing: float32 [1024, 3, 3], P(('comp', 'tgt', 'src')), may hold values from -5 to 5
- near_matrix: bfloat16 [1024, 256, 256], P(('comp', 'tgt', 'src')), may hold values from -0.1875 to 0.1875
Outputs:
- result: float32 [3, 32, 65536], P(None, None, ('comp', 'tgt', 'src'))
Inputs may be any that keep to these rules, and one draw needn't show every extreme that they name: `dest_group`: among the 128 blocks of one device at most 16 name the same target group, and in every draw some device has exactly 16 blocks to one group.
All inputs are finite; a program needn't handle non-finite values.
Results may differ from a plain program's by a relative error of at most 0.0018.
Values may be sent and summed in bfloat16 or wider, within the bound.
No kernel may reach another device: no remote copies, remote signals or barrier semaphores. Data moves between devices by JAX's collectives and lax.ppermute only.
A program may use at most 128 MiB of HBM per device.

v0:
```python
import jax
import jax.numpy as jnp
from jax import lax
from jax.sharding import PartitionSpec as P


def in_blocks(x, dim, length):
    before, after = (x.shape[:dim], x.shape[dim + 1 :])
    return jnp.moveaxis(x.reshape(*before, length, -1, *after), dim, 0)


def sent_and_summed(x, axis, dim):
    parts = in_blocks(x, dim, lax.axis_size(axis))
    arrived = lax.all_to_all(parts, axis, split_axis=0, concat_axis=0, tiled=True)
    return arrived.sum(axis=0)


def body(
    field,
    dest_group,
    src_local,
    ranks,
    mixing,
    v_factor,
    u_factor,
    slot_cluster,
    near_src,
    near_tgt,
    near_mixing,
    near_matrix,
):
    groups = lax.axis_size("tgt")
    shards = lax.axis_size("src")
    pairing = lax.axis_size("comp")
    blocks, rank_width, cluster_size = v_factor.shape
    components, vectors, points = field.shape
    channels = components * vectors
    owned_clusters = points // cluster_size
    slot_count = u_factor.shape[0]
    capacity = slot_count // groups
    targets = owned_clusters * shards
    near_count = near_matrix.shape[0]
    sources = field.reshape(channels, owned_clusters, cluster_size)
    highest = lax.Precision.HIGHEST
    chosen = (src_local[:, None] == jnp.arange(owned_clusters, dtype=jnp.int32)[None, :]).astype(
        jnp.bfloat16
    )
    selected = jnp.einsum(
        "bk,fkp->bfp", chosen, sources, preferred_element_type=jnp.float32
    ).astype(jnp.bfloat16)
    coefficients = jnp.einsum(
        "bfp,brp->bfr", selected, v_factor, preferred_element_type=jnp.float32
    )
    rank_mask = (jnp.arange(rank_width, dtype=jnp.int32)[None, :] < ranks[:, None]).astype(
        jnp.float32
    )
    coefficients = (coefficients * rank_mask[:, None, :]).reshape(
        blocks, components, vectors, rank_width
    )
    mixed_coef = jnp.einsum("bcd,bdsr->bcsr", mixing, coefficients, precision=highest)
    mixed_coef = mixed_coef.reshape(blocks, channels * rank_width).astype(jnp.bfloat16)
    destination = dest_group[:, 0]
    member = (destination[:, None] == jnp.arange(groups, dtype=jnp.int32)[None, :]).astype(
        jnp.int32
    )
    position = jnp.sum(jnp.cumsum(member, axis=0) * member, axis=1) - 1
    slot_of = destination * capacity + position
    placing = (slot_of[:, None] == jnp.arange(slot_count, dtype=jnp.int32)[None, :]).astype(
        jnp.bfloat16
    )
    outgoing = jnp.einsum(
        "bs,bf->sf", placing, mixed_coef, preferred_element_type=jnp.float32
    ).astype(jnp.bfloat16)
    outgoing = outgoing.reshape(groups, capacity, channels * rank_width)
    incoming = lax.all_to_all(outgoing, "tgt", split_axis=0, concat_axis=0, tiled=True)
    near_chosen = (
        near_src[:, None] == jnp.arange(owned_clusters, dtype=jnp.int32)[None, :]
    ).astype(jnp.bfloat16)
    near_inputs = jnp.einsum(
        "nk,fkp->nfp", near_chosen, sources, preferred_element_type=jnp.float32
    ).astype(jnp.bfloat16)
    dense_out = jnp.einsum(
        "nfp,nqp->nfq", near_inputs, near_matrix, preferred_element_type=jnp.float32
    )
    dense_out = dense_out.reshape(near_count, components, vectors, cluster_size)
    mixed_near = jnp.einsum("ncd,ndsq->ncsq", near_mixing, dense_out, precision=highest).reshape(
        near_count, channels, cluster_size
    )
    near_spread = (near_tgt[:, None] == jnp.arange(targets, dtype=jnp.int32)[None, :]).astype(
        jnp.float32
    )
    near_part = jnp.einsum("nt,nfq->ftq", near_spread, mixed_near, precision=highest)
    received = incoming.reshape(slot_count, channels, rank_width)
    contrib = jnp.einsum("sfr,srq->sfq", received, u_factor, preferred_element_type=jnp.float32)
    far_spread = (slot_cluster[:, None] == jnp.arange(targets, dtype=jnp.int32)[None, :]).astype(
        jnp.float32
    )
    far_part = jnp.einsum("st,sfq->ftq", far_spread, contrib, precision=highest)
    partial_value = far_part + near_part
    half_owned = targets // (pairing * shards)
    summed = sent_and_summed(partial_value, ("comp", "src"), 1)
    return summed.reshape(components, vectors, half_owned * cluster_size)


def solution(mesh):
    placed = (
        P(None, None, ("tgt", "src")),
        P(("comp", "tgt", "src"), None),
        P(("comp", "tgt", "src")),
        P(("comp", "tgt", "src")),
        P(("comp", "tgt", "src"), None, None),
        P(("comp", "tgt", "src"), None, None),
        P(("comp", "tgt", "src"), None, None),
        P(("comp", "tgt", "src")),
        P(("comp", "tgt", "src")),
        P(("comp", "tgt", "src")),
        P(("comp", "tgt", "src"), None, None),
        P(("comp", "tgt", "src"), None, None),
    )
    return jax.shard_map(
        body,
        mesh=mesh,
        in_specs=placed,
        out_specs=P(None, None, ("comp", "tgt", "src")),
        check_vma=False,
    )
```

profile of v0, /device:TPU:1, one launch (start us, length us, event | category | flops | bytes accessed | tf_op | source)
XLA Modules:
  0.0 210.8 jit_solution(360051194448593565)
XLA Ops:
  0.0 0.8 fusion.14
  1.0 0.8 select_reduce_fusion
  1.8 0.7 fusion.29
  2.5 0.9 reshape.59
  3.4 0.9 fusion.15
  4.3 2.7 %convolution_convert_fusion.2 = bf16[128,96,256]{2,0,1:T(8,128)(2,1)S(1)} fusion(bf16[96,2,256]{2,1,0:T(2,128)(2,1)S(1)} %reshape.59, s32[128]{0:T(128)} %param.14), kind=kOutput, calls=%fused_computation.7 | convolution fusion | flops 15728896 | bytes 6390272 | tf_op jit(solution)/shard_map/bk,fkp->bfp/dot_general | solution.py:48
  7.0 9.1 %broadcast_multiply_fusion = f32[128,96,64]{1,2,0:T(8,128)} fusion(f32[128,64]{1,0:T(8,128)S(1)} %fusion.15, bf16[128,64,256]{2,1,0:T(8,128)(2,1)S(1)} %copy-done.2, bf16[128,96,256]{2,0,1:T(8,128)(2,1)S(1)} %convolution_convert_fusion.2), kind=kOutput, calls=%fused_computation.8 | convolution fusion | flops 403439616 | bytes 13664256 | tf_op jit(solution)/shard_map/bfp,brp->bfr/dot_general | solution.py:51
  16.1 5.3 %copy.26 = f32[128,96,64]{0,2,1:T(8,128)} copy(f32[128,96,64]{1,2,0:T(8,128)} %broadcast_multiply_fusion) | data formatting | bytes 6291456 | tf_op jit(solution)/shard_map/mul | solution.py:57
  21.5 7.7 %copy.27 = f32[128,3,32,64]{3,1,2,0:T(4,128)} copy(f32[128,3,32,64]{0,3,2,1:T(8,128)} %bitcast.47) | data formatting | bytes 6291456 | tf_op jit(solution)/shard_map/reshape | solution.py:57
  29.3 18.0 %fusion.4 = bf16[128,3,32,64]{3,1,2,0:T(4,128)(2,1)} fusion(f32[128,3,32,64]{3,1,2,0:T(4,128)} %copy.27, f32[128,3,3,1]{2,1,3,0:T(4,128)S(1)} %copy.38), kind=kOutput, calls=%fused_computation.6 | convolution fusion | flops 29097984 | bytes 4723200 | tf_op jit(solution)/shard_map/bcd,bdsr->bcsr/dot_general | solution.py:60
  47.3 5.9 %copy.29 = bf16[128,3,32,64]{0,3,2,1:T(8,128)(2,1)S(1)} copy(bf16[128,3,32,64]{3,1,2,0:T(4,128)(2,1)} %fusion.4) | data formatting | bytes 3145728 | tf_op jit(solution)/shard_map/convert_element_type | solution.py:61
  53.3 2.8 %convolution_convert_fusion = bf16[256,6144]{1,0:T(8,128)(2,1)} fusion(bf16[128,6144]{0,1:T(8,128)(2,1)S(1)} %bitcast.48, s32[128]{0:T(128)S(1)} %fusion.29), kind=kOutput, calls=%fused_computation.2 | convolution fusion | flops 404291584 | bytes 4719104 | tf_op jit(solution)/shard_map/bs,bf->sf/dot_general | solution.py:71
  56.1 7.6 %all-to-all-start = ((bf16[16,16,6144]{2,1,0:T(8,128)(2,1)}), bf16[16,16,6144]{2,1,0:T(8,128)(2,1)}, u32[]{:S(2)}, u32[]{:S(2)}) async-start(bf16[16,16,6144]{2,1,0:T(8,128)(2,1)} %bitcast.46), calls=%async_computation | async-start | bytes 6291456 | tf_op jit(solution)/shard_map/all_to_all | solution.py:75
  63.7 0.3 convolution_convert_fusion.3
  64.1 0.3 fusion.9
  64.4 1.2 convolution_bitcast_fusion
  65.7 44.8 %all-to-all-done = bf16[16,16,6144]{2,1,0:T(8,128)(2,1)} async-done(((bf16[16,16,6144]{2,1,0:T(8,128)(2,1)}), bf16[16,16,6144]{2,1,0:T(8,128)(2,1)}, u32[]{:S(2)}, u32[]{:S(2)}) %all-to-all-start) | async-done | bytes 3145760 | tf_op jit(solution)/shard_map/all_to_all | solution.py:75
  110.4 9.6 %reshape.62 = bf16[256,96,64]{2,1,0:T(8,128)(2,1)} reshape(bf16[16,16,6144]{2,1,0:T(8,128)(2,1)} %all-to-all-done) | data formatting | bytes 6291456 | tf_op jit(solution)/shard_map/reshape | solution.py:93
  120.1 16.9 %fusion.32 = f32[256,96,256]{2,1,0:T(8,128)} fusion(bf16[256,96,64]{2,1,0:T(8,128)(2,1)} %reshape.62, bf16[256,64,256]{2,1,0:T(8,128)(2,1)} %param.18), kind=kOutput, calls=%fused_computation.41 | convolution fusion | flops 805306368 | bytes 36700160 | tf_op jit(solution)/shard_map/sfr,srq->sfq/dot_general | solution.py:94
  137.0 21.3 %fusion = f32[96,256,16]{1,2,0:T(8,128)S(1)} fusion(f32[256,96,256]{2,1,0:T(8,128)} %fusion.32, s32[256]{0:T(256)S(1)} %copy-done.5), kind=kOutput, calls=%fused_computation | convolution fusion | flops 1207963648 | bytes 26739712 | tf_op jit(solution)/shard_map/st,sfq->ftq/dot_general | solution.py:98
  158.3 1.0 add_bitcast_fusion
  159.3 0.9 copy.37
  160.2 49.9 %all_to_all.10 = f32[16,96,1,256]{3,1,2,0:T(8,128)S(1)} all-to-all(f32[16,96,1,256]{3,1,2,0:T(8,128)S(1)} %copy.37), channel_id=1, replica_groups=mesh['comp'=2,'tgt'=16,'src'=8] {'comp','src'}, dimensions={0} | all-to-all | bytes 3145728 | tf_op jit(solution)/shard_map/all_to_all | solution.py:14
  210.1 0.7 reduce_sum.19
  (19 shorter events, 0.5 us)
Async XLA Ops:
  0.0 64.1 %copy-start = (bf16[4,256,256]{2,1,0:T(8,128)(2,1)S(1)}, bf16[4,256,256]{2,1,0:T(8,128)(2,1)}, u32[]{:S(2)}) copy-start(bf16[4,256,256]{2,1,0:T(8,128)(2,1)} %param.23) | copy-start | bytes 1572868
  3.4 3.6 %copy-start.2 = (bf16[128,64,256]{2,1,0:T(8,128)(2,1)S(1)}, bf16[128,64,256]{2,1,0:T(8,128)(2,1)}, u32[]{:S(2)}) copy-start(bf16[128,64,256]{2,1,0:T(8,128)(2,1)} %param.17) | copy-start | bytes 12582916
  21.4 7.7 %copy-start.4 = (f32[128,3,3]{0,2,1:T(4,128)S(1)}, f32[128,3,3]{0,2,1:T(4,128)}, u32[]{:S(2)}) copy-start(f32[128,3,3]{0,2,1:T(4,128)} %param.16) | copy-start | bytes 13828
  53.3 10.4 %copy-start.7 = (s32[4]{0:T(128)S(1)}, s32[4]{0:T(128)}, u32[]{:S(2)}) copy-start(s32[4]{0:T(128)} %param.20) | copy-start | bytes 52
  53.3 11.0 %copy-start.3 = (f32[4,3,3]{2,0,1:T(4,128)S(1)}, f32[4,3,3]{2,0,1:T(4,128)}, u32[]{:S(2)}) copy-start(f32[4,3,3]{2,0,1:T(4,128)} %param.22) | copy-start | bytes 436
  56.1 54.3 %all-to-all-start = ((bf16[16,16,6144]{2,1,0:T(8,128)(2,1)}), bf16[16,16,6144]{2,1,0:T(8,128)(2,1)}, u32[]{:S(2)}, u32[]{:S(2)}) async-start(bf16[16,16,6144]{2,1,0:T(8,128)(2,1)} %bitcast.46), calls=%async_computation | async-start | bytes 6291456 | tf_op jit(solution)/shard_map/all_to_all | solution.py:75
  120.1 16.9 %copy-start.5 = (s32[256]{0:T(256)S(1)}, s32[256]{0:T(256)}, u32[]{:S(2)}) copy-start(s32[256]{0:T(256)} %param.19) | copy-start | bytes 3076
  137.0 21.3 %copy-start.6 = (s32[4]{0:T(128)S(1)}, s32[4]{0:T(128)}, u32[]{:S(2)}) copy-start(s32[4]{0:T(128)} %param.21) | copy-start | bytes 52
  137.0 73.8 %copy-start.1 = (bf16[4,256,256]{2,1,0:T(8,128)(2,1)S(1)}, bf16[4,256,256]{2,1,0:T(8,128)(2,1)}, u32[]{:S(2)}) copy-start(bf16[4,256,256]{2,1,0:T(8,128)(2,1)} %param.23) | copy-start | bytes 1572868
where the time goes:
time: 212 us; the launch traced here: 211 us
  matrix products  73.5 us (35%)
  blocking collectives  49.9 us (24%)
  waiting for transfers between devices  44.8 us (21%)
  local copies, waits for them, and re-layouts  30.7 us (14%)
  starting transfers between devices  7.63 us (4%)
  other arithmetic  4.08 us (2%)
    all_to_all x1, blocking collectives, sent_and_summed(): lax.all_to_all(parts, axis, split_axis=0, concat_axis=0, tiled=True)  49.9 us
    all_to_all x1, waiting for transfers between devices, body(): lax.all_to_all(outgoing, 'tgt', split_axis=0, concat_axis=0, tiled=True)  44.8 us
    dot_general x1, matrix products, body(): far_part = jnp.einsum('st,sfq->ftq', far_spread, contrib, precision=highest)  21.3 us
    dot_general x1, matrix products, body(): jnp.einsum('bcd,bdsr->bcsr', mixing, coefficients, precision=highest)  18 us
    dot_general x1, matrix products, body(): jnp.einsum('sfr,srq->sfq', received, u_factor, preferred_element_type=jnp...  16.9 us
    reshape x1, local copies, waits for them, and re-layouts, body(): received = incoming.reshape(slot_count, channels, rank_width)  9.63 us
    dot_general x1, matrix products, body(): jnp.einsum('bfp,brp->bfr', selected, v_factor, preferred_element_type=jnp...  9.06 us
    reshape x1, local copies, waits for them, and re-layouts, body(): (coefficients * rank_mask[:, None, :]).reshape(blocks, components, vector...  7.7 us
  transfers between devices with their start and end apart: 1, of which 1 were waited for; matrix products, arithmetic and copies ran while one was open for 1% of the time, Pallas kernels for 0%

commit v1 on v0

v1 whole, which is shorter than its diff:
```python
import functools

import jax
import jax.numpy as jnp
from jax import lax
from jax.experimental import pallas as pl
from jax.experimental.pallas import tpu as pltpu
from jax.sharding import PartitionSpec as P

SUB = 8
QUAD = 4


def spread(values, lane, width):
    out = values[-1]
    for t in range(len(values) - 2, -1, -1):
        out = jnp.where(lane < (t + 1) * width, values[t], out)
    return out


def source_kernel(
    comps, groups, capacity, dest, src, ranks, mixing, field, v, out, x, slots, counts
):
    step = pl.program_id(0)
    per_step = out.shape[0]
    blocks, rank_width, cluster = v.shape
    channels = out.shape[1]
    rhs = channels // comps
    owned = x.shape[0] // channels

    @pl.when(step == 0)
    def _():
        for s in range(owned):
            x[s * channels : (s + 1) * channels, :] = field[:, s * cluster : (s + 1) * cluster]
        for g in range(groups):
            counts[g] = 0

        def place(b, carry):
            g = dest[b]
            k = counts[g]
            counts[g] = k + 1
            slots[g * capacity + k] = b
            return carry

        lax.fori_loop(0, blocks, place, 0, unroll=8)

    width = QUAD * rank_width
    lane = lax.broadcasted_iota(jnp.int32, (SUB, width), 1)
    within = lane & (rank_width - 1)

    def one_group(n, carry):
        g = step * per_step + n
        count = counts[g]
        for q in range(capacity // QUAD):
            cols = slice(q * width, (q + 1) * width)

            @pl.when(count > q * QUAD)
            def _():
                first = g * capacity + q * QUAD
                full = [count > q * QUAD + t for t in range(QUAD)]
                ids = [jnp.where(full[t], slots[first + t], 0) for t in range(QUAD)]
                basis = jnp.concatenate([v[b] for b in ids], axis=0)
                y = lax.dot_general(
                    x[...], basis, (((1,), (1,)), ((), ())), preferred_element_type=jnp.float32
                ).reshape(owned, comps, rhs // SUB, SUB, width)
                which = spread([src[b] for b in ids], lane, rank_width)
                picked = y[0]
                for s in range(1, owned):
                    picked = jnp.where(which == s, y[s], picked)
                limit = spread(
                    [jnp.where(full[t], ranks[ids[t]], 0) for t in range(QUAD)], lane, rank_width
                )
                kept = within < limit
                for e in range(comps):
                    total = None
                    for e2 in range(comps):
                        entry = (e * comps + e2) * blocks
                        m = spread([mixing[entry + b] for b in ids], lane, rank_width)
                        m = jnp.where(kept, m, 0.0)
                        term = m * picked[e2]
                        total = term if total is None else total + term
                    out[n, e * rhs : (e + 1) * rhs, cols] = total.reshape(rhs, width).astype(
                        out.dtype
                    )

            @pl.when(count <= q * QUAD)
            def _():
                out[n, :, cols] = jnp.zeros((channels, width), out.dtype)

        return carry

    lax.fori_loop(0, per_step, one_group, 0)


def target_kernel(
    comps, place, slot_cluster, near_src, near_tgt, near_mixing, where, field, near, u, sent, mine, other
):
    step = pl.program_id(0)
    per_step, channels, lanes = sent.shape
    slot_rows, rank_width, cluster = u.shape
    capacity = slot_rows // per_step
    width = QUAD * rank_width
    near_count = near.shape[0]
    rhs = channels // comps
    core = where[0]

    def add(w, value):
        row, own = place(w, core)

        @pl.when(own)
        def _():
            mine[row] += value

        @pl.when(jnp.logical_not(own))
        def _():
            other[row] += value

    @pl.when(step == 0)
    def _():
        mine[...] = jnp.zeros_like(mine)
        other[...] = jnp.zeros_like(other)
        for n in range(near_count):
            begin = pl.multiple_of(near_src[n] * cluster, cluster)
            y = lax.dot_general(
                field[:, pl.ds(begin, cluster)],
                near[n],
                (((1,), (1,)), ((), ())),
                preferred_element_type=jnp.float32,
            )
            parts = [y[e * rhs : (e + 1) * rhs] for e in range(comps)]
            rows = []
            for e in range(comps):
                total = None
                for e2 in range(comps):
                    term = near_mixing[(e * comps + e2) * near_count + n] * parts[e2]
                    total = term if total is None else total + term
                rows.append(total)
            add(near_tgt[n], jnp.concatenate(rows, axis=0))

    lane = lax.broadcasted_iota(jnp.int32, (1, width), 1)
    for n in range(per_step):
        for q in range(capacity // QUAD):
            a = sent[n, :, q * width : (q + 1) * width]
            first = n * capacity + q * QUAD
            basis = u[first : first + QUAD].reshape(width, cluster)
            for t in range(QUAD):
                inside = (lane >= t * rank_width) & (lane < (t + 1) * rank_width)
                one = jnp.where(inside, a, jnp.zeros_like(a))
                far = jnp.dot(one, basis, preferred_element_type=jnp.float32)
                add(slot_cluster[step * slot_rows + first + t], far)


def body(
    field,
    dest_group,
    src_local,
    ranks,
    mixing,
    v_factor,
    u_factor,
    slot_cluster,
    near_src,
    near_tgt,
    near_mixing,
    near_matrix,
):
    groups = lax.axis_size("tgt")
    shards = lax.axis_size("src")
    pairing = lax.axis_size("comp")
    blocks, rank_width, cluster = v_factor.shape
    comps, vectors, points = field.shape
    channels = comps * vectors
    owned = points // cluster
    slot_count = u_factor.shape[0]
    capacity = slot_count // groups
    near_count = near_matrix.shape[0]
    cores = 2
    chips = pairing * shards // cores
    smem = pl.BlockSpec(memory_space=pltpu.SMEM)

    x = field.reshape(channels, points)
    per_step = 4
    outgoing = pl.pallas_call(
        functools.partial(source_kernel, comps, groups, capacity),
        grid=(groups // per_step,),
        out_shape=jax.ShapeDtypeStruct((groups, channels, capacity * rank_width), jnp.bfloat16),
        in_specs=[smem] * 4
        + [
            pl.BlockSpec((channels, points), lambda i: (0, 0)),
            pl.BlockSpec(v_factor.shape, lambda i: (0, 0, 0), pipeline_mode=pl.Buffered(1)),
        ],
        out_specs=pl.BlockSpec((per_step, channels, capacity * rank_width), lambda i: (i, 0, 0)),
        scratch_shapes=[
            pltpu.VMEM((owned * channels, cluster), jnp.bfloat16),
            pltpu.SMEM((slot_count,), jnp.int32),
            pltpu.SMEM((groups,), jnp.int32),
        ],
        compiler_params=pltpu.CompilerParams(vmem_limit_bytes=48 << 20),
        name="source",
    )(
        dest_group[:, 0],
        src_local,
        ranks,
        mixing.transpose(1, 2, 0).reshape(-1),
        x,
        v_factor,
    )
    incoming = lax.all_to_all(outgoing, "tgt", split_axis=0, concat_axis=0, tiled=True)

    def place(w, core):
        c, j = w // shards, w % shards
        return (j // cores) * pairing + c, (j % cores) == core

    core = (lax.axis_index("src") % cores).astype(jnp.int32).reshape(1)
    steps = 8
    senders = groups // steps
    half = jax.ShapeDtypeStruct((chips, channels, cluster), jnp.float32)
    whole = pl.BlockSpec(half.shape, lambda i: (0, 0, 0))
    mine, other = pl.pallas_call(
        functools.partial(target_kernel, comps, place),
        grid=(steps,),
        out_shape=[half, half],
        in_specs=[smem] * 5
        + [
            pl.BlockSpec((channels, points), lambda i: (0, 0)),
            pl.BlockSpec(near_matrix.shape, lambda i: (0, 0, 0)),
            pl.BlockSpec((senders * capacity, rank_width, cluster), lambda i: (i, 0, 0)),
            pl.BlockSpec((senders, channels, capacity * rank_width), lambda i: (i, 0, 0)),
        ],
        out_specs=[whole, whole],
        compiler_params=pltpu.CompilerParams(vmem_limit_bytes=48 << 20),
        name="target",
    )(
        slot_cluster,
        near_src,
        near_tgt,
        near_mixing.transpose(1, 2, 0).reshape(-1),
        core,
        x,
        near_matrix,
        u_factor,
        incoming,
    )
    swapped = lax.ppermute(other, "src", [(j, j ^ 1) for j in range(shards)])
    sums = (mine + swapped).astype(jnp.bfloat16)
    lines = [
        [c * shards + h * cores + k for h in range(shards // cores) for c in range(pairing)]
        for k in range(cores)
    ]
    parts = lax.all_to_all(
        sums, ("comp", "src"), split_axis=0, concat_axis=0, tiled=True, axis_index_groups=lines
    )
    return parts.astype(jnp.float32).sum(axis=0).reshape(comps, vectors, cluster)


def solution(mesh):
    every = ("comp", "tgt", "src")
    placed = (
        P(None, None, ("tgt", "src")),
        P(every, None),
        P(every),
        P(every),
        P(every, None, None),
        P(every, None, None),
        P(every, None, None),
        P(every),
        P(every),
        P(every),
        P(every, None, None),
        P(every, None, None),
    )
    return jax.shard_map(
        body,
        mesh=mesh,
        in_specs=placed,
        out_specs=P(None, None, every),
        check_vma=False,
    )
```

time: 212 us -> 147 us (0.69)
  matrix products: 73.5 us -> 0 us
  Pallas kernels: 0 us -> 61 us
  blocking collectives: 49.9 us -> 22.1 us
  local copies, waits for them, and re-layouts: 30.7 us -> 4.81 us
  other arithmetic: 4.08 us -> 0.83 us
  waiting for transfers between devices: 44.8 us -> 47.3 us
  starting transfers between devices: 7.63 us -> 10.1 us
    dot_general x10 -> x0, matrix products: 73.5 us -> none  [the longest x1 21.3 us: body(): far_part = jnp.einsum('st,sfq->ftq', far_spread, contrib, precision=highest)]
    pallas_call x0 -> x2, Pallas kernels: none -> 61 us  [the longest x1 47.6 us: body(): pl.pallas_call(functools.partial(target_kernel, comps, place), grid=(step...]
    all_to_all x1, blocking collectives: 49.9 us -> 22.1 us  [body(): lax.all_to_all(sums, ('comp', 'src'), split_axis=0, concat_axis=0, tiled=...]
    reshape x3 -> x2, local copies, waits for them, and re-layouts: 18.3 us -> 0.79 us  [the longest x1 0.7 us: body(): mixing.transpose(1, 2, 0).reshape(-1)]
    convert_element_type x1 -> x0, local copies, waits for them, and re-layouts: 5.95 us -> none  [body(): mixed_coef.reshape(blocks, channels * rank_width).astype(jnp.bfloat16)]
    mul x1 -> x0, local copies, waits for them, and re-layouts: 5.34 us -> none  [body(): coefficients * rank_mask[:, None, :]]
    unnamed x17 -> x20, local copies, waits for them, and re-layouts: 0.21 us -> 3.92 us
    ppermute x0 -> x1, starting transfers between devices: none -> 2.35 us  [body(): swapped = lax.ppermute(other, 'src', [(j, j ^ 1) for j in range(shards)])]
  transfers between devices with their start and end apart: 1 -> 2, of which waited for: 1 -> 2; matrix products, arithmetic and copies ran while one was open for 1% -> 0% of each run, Pallas kernels for 0% -> 0%
where the time goes in v1:
time: 147 us; the launch traced here: 146 us
  Pallas kernels  61 us (41%)
  waiting for transfers between devices  47.3 us (32%)
  blocking collectives  22.1 us (15%)
  starting transfers between devices  10.1 us (7%)
  local copies, waits for them, and re-layouts  4.81 us (3%)
    pallas_call x1, Pallas kernels, body(): pl.pallas_call(functools.partial(target_kernel, comps, place), grid=(step...  47.6 us
    all_to_all x1, waiting for transfers between devices, body(): lax.all_to_all(outgoing, 'tgt', split_axis=0, concat_axis=0, tiled=True)  45.4 us
    all_to_all x1, blocking collectives, body(): lax.all_to_all(sums, ('comp', 'src'), split_axis=0, concat_axis=0, tiled=...  22.1 us
    pallas_call x1, Pallas kernels, body(): pl.pallas_call(functools.partial(source_kernel, comps, groups, capacity),...  13.4 us
    all_to_all x1, starting transfers between devices, body(): lax.all_to_all(outgoing, 'tgt', split_axis=0, concat_axis=0, tiled=True)  7.76 us
    unnamed x20, local copies, waits for them, and re-layouts  3.92 us
  transfers between devices with their start and end apart: 2, of which 2 were waited for; matrix products, arithmetic and copies ran while one was open for 0% of the time, Pallas kernels for 0%

profile of v1, /device:TPU:1, one launch (start us, length us, event | category | flops | bytes accessed | tf_op | source)
XLA Modules:
  0.0 146.2 jit_solution(4810632464161374021)
XLA Ops:
  0.0 0.7 reshape.18.mixing
  0.7 0.9 copy-done.1
  1.6 0.7 copy-done.4
  2.3 0.7 copy-done.5
  2.9 0.7 copy-done.6
  3.6 13.4 %source.1 = bf16[16,96,1024]{2,1,0:T(8,128)(2,1)} custom-call(s32[128]{0:T(128)S(1)} %bitcast.8, s32[128]{0:T(128)S(1)} %copy-done.5, s32[128]{0:T(128)S(1)} %copy-done.6, f32[1152]{0:T(1024)S(1)} %reshape.18.mixing, bf16[96,512]{1,0:T(8,128)(2,1)S(1)} %bitcast.6, bf16[128,64,256]{2,1,0:T(8,128)(2,1)} %v.1), custom_call_target="tpu_custom_call" | custom-call | tf_op jit(solution)/shard_map/source/pallas_call | solution.py:183
  17.0 0.0 copy-start.7
  17.0 0.0 copy-start.8
  17.0 7.8 %all-to-all-start = ((bf16[16,96,1024]{2,1,0:T(8,128)(2,1)}), bf16[16,96,1024]{2,1,0:T(8,128)(2,1)S(1)}, u32[]{:S(2)}, u32[]{:S(2)}) async-start(bf16[16,96,1024]{2,1,0:T(8,128)(2,1)} %source.1), calls=%async_computation | async-start | bytes 6291456 | tf_op jit(solution)/shard_map/all_to_all | solution.py:208
  24.8 0.0 copy-done.9
  24.8 0.1 copy.13
  24.9 0.1 reshape.15.near_mixing
  25.0 45.4 %all-to-all-done.sent = bf16[16,96,1024]{2,1,0:T(8,128)(2,1)S(1)} async-done(((bf16[16,96,1024]{2,1,0:T(8,128)(2,1)}), bf16[16,96,1024]{2,1,0:T(8,128)(2,1)S(1)}, u32[]{:S(2)}, u32[]{:S(2)}) %all-to-all-start) | async-done | bytes 3145760 | tf_op jit(solution)/shard_map/all_to_all | solution.py:208
  70.3 0.0 copy-done.2
  70.3 0.0 copy-done.3
  70.4 0.0 copy-done.7
  70.4 0.0 copy-start
  70.4 1.0 copy-done
  71.4 47.6 %target.1 = (f32[8,96,256]{2,1,0:T(8,128)S(1)}, f32[8,96,256]{2,1,0:T(8,128)S(1)}) custom-call(s32[256]{0:T(256)S(1)} %copy-done.3, s32[4]{0:T(128)S(1)} %copy-done.7, s32[4]{0:T(128)S(1)} %copy-done.8, f32[36]{0:T(128)S(1)} %reshape.15.near_mixing, s32[1]{0:T(128)} %bitcast.1.where, bf16[96,512]{1,0:T(8,128)(2,1)S(1)} %bitcast.7, ...), custom_call_target="tpu_custom_call" | custom-call | tf_op jit(solution)/shard_map/target/pallas_call | solution.py:219
  119.0 2.3 %collective-permute-start = (f32[8,96,256]{2,1,0:T(8,128)S(1)}, f32[8,96,256]{2,1,0:T(8,128)S(1)}, u32[]{:S(2)}, u32[]{:S(2)}) collective-permute-start(f32[8,96,256]{2,1,0:T(8,128)S(1)} %get-tuple-element.8), channel_id=1, source_target_pairs={{0,1},{1,0},{2,3},{3,2},{4,5},{5,4},{6,7},{7,6},{8,9},{9,8},{10,11... | collective-permute-start | bytes 2359304 | tf_op jit(solution)/shard_map/ppermute | solution.py:244
  121.3 1.9 %collective-permute-done = f32[8,96,256]{2,1,0:T(8,128)S(1)} collective-permute-done((f32[8,96,256]{2,1,0:T(8,128)S(1)}, f32[8,96,256]{2,1,0:T(8,128)S(1)}, u32[]{:S(2)}, u32[]{:S(2)}) %collective-permute-start) | collective-permute-done | bytes 786464 | tf_op jit(solution)/shard_map/ppermute | solution.py:244
  123.2 0.1 add_convert_fusion
  123.4 22.1 %all_to_all.10 = bf16[8,96,256]{2,1,0:T(8,128)(2,1)S(1)} all-to-all(bf16[8,96,256]{2,1,0:T(8,128)(2,1)S(1)} %add_convert_fusion), channel_id=1, replica_groups={{0,128,2,130,4,132,6,134},{1,129,3,131,5,133,7,135},{8,136,10,138,12,14..., dimensions={0} | all-to-all | bytes 786432 | tf_op jit(solution)/shard_map/all_to_all | solution.py:250
  145.5 0.7 convert_reduce_fusion
  (8 shorter events, 0.0 us)
Async XLA Ops:
  0.7 0.9 copy-start.1
  1.6 0.7 copy-start.4
  2.2 0.7 copy-start.5
  2.9 0.7 copy-start.6
  16.9 7.8 %copy-start.9 = (f32[4,3,3]{2,0,1:T(4,128)S(1)}, f32[4,3,3]{2,0,1:T(4,128)}, u32[]{:S(2)}) copy-start(f32[4,3,3]{2,0,1:T(4,128)} %param.22) | copy-start | bytes 436
  16.9 53.4 %copy-start.2 = (bf16[3,32,512]{2,1,0:T(8,128)(2,1)S(1)}, bf16[3,32,512]{2,1,0:T(8,128)(2,1)}, u32[]{:S(2)}) copy-start(bf16[3,32,512]{2,1,0:T(8,128)(2,1)} %param.12) | copy-start | bytes 294916
  16.9 53.4 %copy-start.3 = (s32[256]{0:T(256)S(1)}, s32[256]{0:T(256)}, u32[]{:S(2)}) copy-start(s32[256]{0:T(256)} %slot_cluster.1) | copy-start | bytes 3076
  17.0 53.4 %copy-start.7 = (s32[4]{0:T(128)S(1)}, s32[4]{0:T(128)}, u32[]{:S(2)}) copy-start(s32[4]{0:T(128)} %near_src.1) | copy-start | bytes 52
  17.0 53.4 %copy-start.8 = (s32[4]{0:T(128)S(1)}, s32[4]{0:T(128)}, u32[]{:S(2)}) copy-start(s32[4]{0:T(128)} %near_tgt.1) | copy-start | bytes 52
  17.0 53.4 %all-to-all-start = ((bf16[16,96,1024]{2,1,0:T(8,128)(2,1)}), bf16[16,96,1024]{2,1,0:T(8,128)(2,1)S(1)}, u32[]{:S(2)}, u32[]{:S(2)}) async-start(bf16[16,96,1024]{2,1,0:T(8,128)(2,1)} %source.1), calls=%async_computation | async-start | bytes 6291456 | tf_op jit(solution)/shard_map/all_to_all | solution.py:208
  70.4 1.0 copy-start
  119.0 4.3 %collective-permute-start = (f32[8,96,256]{2,1,0:T(8,128)S(1)}, f32[8,96,256]{2,1,0:T(8,128)S(1)}, u32[]{:S(2)}, u32[]{:S(2)}) collective-permute-start(f32[8,96,256]{2,1,0:T(8,128)S(1)} %get-tuple-element.8), channel_id=1, source_target_pairs={{0,1},{1,0},{2,3},{3,2},{4,5},{5,4},{6,7},{7,6},{8,9},{9,8},{10,11... | collective-permute-start | bytes 2359304 | tf_op jit(solution)/shard_map/ppermute | solution.py:244

commit v2 on v1

v2 whole, which is shorter than its diff:
```python
import functools

import jax
import jax.numpy as jnp
from jax import lax
from jax.experimental import pallas as pl
from jax.experimental.pallas import tpu as pltpu
from jax.sharding import PartitionSpec as P

SUB = 8
QUAD = 4


def spread(values, lane, width):
    out = values[-1]
    for t in range(len(values) - 2, -1, -1):
        out = jnp.where(lane < (t + 1) * width, values[t], out)
    return out


def source_kernel(
    comps,
    dest_hbm,
    src_hbm,
    ranks_hbm,
    mixing_hbm,
    field_hbm,
    v_hbm,
    out,
    dest,
    src,
    ranks,
    mixing,
    field,
    v,
    x,
    slots,
    counts,
    small_sem,
    big_sem,
):
    step = pl.program_id(0)
    per_step = out.shape[0]
    blocks, rank_width, cluster = v.shape
    channels = out.shape[1]
    rhs = channels // comps
    owned = x.shape[0] // channels
    groups = counts.shape[0]
    capacity = slots.shape[0] // groups

    @pl.when(step == 0)
    def _():
        small = [
            pltpu.make_async_copy(a, b, small_sem.at[n])
            for n, (a, b) in enumerate(
                ((dest_hbm, dest), (src_hbm, src), (ranks_hbm, ranks), (field_hbm, field))
            )
        ]
        small += [
            pltpu.make_async_copy(
                mixing_hbm.at[e, e2], mixing.at[e * comps + e2], small_sem.at[4 + e * comps + e2]
            )
            for e in range(comps)
            for e2 in range(comps)
        ]
        big = pltpu.make_async_copy(v_hbm, v, big_sem)
        for copy in small:
            copy.start()
        big.start()
        for g in range(groups):
            counts[g] = 0
        for copy in small:
            copy.wait()
        for s in range(owned):
            x[s * channels : (s + 1) * channels, :] = field[:, s * cluster : (s + 1) * cluster]

        def put(b, carry):
            g = dest[b]
            k = counts[g]
            counts[g] = k + 1
            slots[g * capacity + k] = b
            return carry

        lax.fori_loop(0, blocks, put, 0, unroll=8)
        big.wait()

    width = QUAD * rank_width
    lane = lax.broadcasted_iota(jnp.int32, (SUB, width), 1)
    within = lane & (rank_width - 1)

    def one_group(n, carry):
        g = step * per_step + n
        count = counts[g]
        for q in range(capacity // QUAD):
            cols = slice(q * width, (q + 1) * width)
            first = g * capacity + q * QUAD
            full = [count > q * QUAD + t for t in range(QUAD)]
            ids = [jnp.where(full[t], slots[first + t], 0) for t in range(QUAD)]
            basis = jnp.concatenate([v[b] for b in ids], axis=0)
            y = lax.dot_general(
                x[...], basis, (((1,), (1,)), ((), ())), preferred_element_type=jnp.float32
            ).reshape(owned, comps, rhs // SUB, SUB, width)
            which = spread([src[b] for b in ids], lane, rank_width)
            picked = y[0]
            for s in range(1, owned):
                picked = jnp.where(which == s, y[s], picked)
            limit = spread(
                [jnp.where(full[t], ranks[ids[t]], 0) for t in range(QUAD)], lane, rank_width
            )
            kept = within < limit
            for e in range(comps):
                total = None
                for e2 in range(comps):
                    m = spread([mixing[e * comps + e2, b] for b in ids], lane, rank_width)
                    m = jnp.where(kept, m, 0.0)
                    term = m * picked[e2]
                    total = term if total is None else total + term
                out[n, e * rhs : (e + 1) * rhs, cols] = total.reshape(rhs, width).astype(out.dtype)
        return carry

    lax.fori_loop(0, per_step, one_group, 0)


def target_kernel(
    comps,
    place,
    clusters_hbm,
    near_src_hbm,
    near_tgt_hbm,
    near_mixing_hbm,
    field_hbm,
    near_hbm,
    u,
    sent,
    mine,
    other,
    clusters,
    near_src,
    near_tgt,
    near_mixing,
    field,
    near,
    total_by_row,
    sems,
):
    step = pl.program_id(0)
    per_step, channels, lanes = sent.shape
    slot_rows, rank_width, cluster = u.shape
    capacity = slot_rows // per_step
    width = QUAD * rank_width
    near_count = near.shape[0]
    rhs = channels // comps
    rows = mine.shape[0]

    def add(w, value):
        row, own = place(w)
        total_by_row[jnp.where(own, row, row + rows)] += value

    @pl.when(step == 0)
    def _():
        copies = [
            pltpu.make_async_copy(a, b, sems.at[n])
            for n, (a, b) in enumerate(
                (
                    (clusters_hbm, clusters),
                    (near_src_hbm, near_src),
                    (near_tgt_hbm, near_tgt),
                    (near_mixing_hbm, near_mixing),
                    (field_hbm, field),
                    (near_hbm, near),
                )
            )
        ]
        for copy in copies:
            copy.start()
        total_by_row[...] = jnp.zeros_like(total_by_row)
        for copy in copies:
            copy.wait()
        for n in range(near_count):
            begin = pl.multiple_of(near_src[n] * cluster, cluster)
            y = lax.dot_general(
                field[:, pl.ds(begin, cluster)],
                near[n],
                (((1,), (1,)), ((), ())),
                preferred_element_type=jnp.float32,
            )
            parts = [y[e * rhs : (e + 1) * rhs] for e in range(comps)]
            mixed = []
            for e in range(comps):
                total = None
                for e2 in range(comps):
                    term = near_mixing[e, n : n + 1, e2 : e2 + 1] * parts[e2]
                    total = term if total is None else total + term
                mixed.append(total)
            add(near_tgt[n], jnp.concatenate(mixed, axis=0))

    lane = lax.broadcasted_iota(jnp.int32, (1, width), 1)
    inside = [(lane >= t * rank_width) & (lane < (t + 1) * rank_width) for t in range(QUAD)]
    for n in range(per_step):
        for q in range(capacity // QUAD):
            a = sent[n, :, q * width : (q + 1) * width]
            first = n * capacity + q * QUAD
            basis = u[first : first + QUAD].reshape(width, cluster)
            one = jnp.concatenate([jnp.where(m, a, jnp.zeros_like(a)) for m in inside], axis=0)
            far = jnp.dot(one, basis, preferred_element_type=jnp.float32)
            for t in range(QUAD):
                add(
                    clusters[step * slot_rows + first + t],
                    far[t * channels : (t + 1) * channels],
                )

    @pl.when(step == pl.num_programs(0) - 1)
    def _():
        mine[...] = total_by_row[:rows]
        other[...] = total_by_row[rows:]


def body(
    field,
    dest_group,
    src_local,
    ranks,
    mixing,
    v_factor,
    u_factor,
    slot_cluster,
    near_src,
    near_tgt,
    near_mixing,
    near_matrix,
):
    groups = lax.axis_size("tgt")
    shards = lax.axis_size("src")
    pairing = lax.axis_size("comp")
    blocks, rank_width, cluster = v_factor.shape
    comps, vectors, points = field.shape
    channels = comps * vectors
    owned = points // cluster
    slot_count = u_factor.shape[0]
    capacity = slot_count // groups
    near_count = near_matrix.shape[0]
    cores = 2
    chips = pairing * shards // cores
    kept = functools.partial(pltpu.with_memory_space_constraint, memory_space=pltpu.HBM)
    hbm = pl.BlockSpec(memory_space=pltpu.HBM)

    x = kept(field.reshape(channels, points))
    per_step = 4
    outgoing = pl.pallas_call(
        functools.partial(source_kernel, comps),
        grid=(groups // per_step,),
        out_shape=jax.ShapeDtypeStruct((groups, channels, capacity * rank_width), jnp.bfloat16),
        in_specs=[hbm] * 6,
        out_specs=pl.BlockSpec((per_step, channels, capacity * rank_width), lambda i: (i, 0, 0)),
        scratch_shapes=[
            pltpu.SMEM((blocks,), jnp.int32),
            pltpu.SMEM((blocks,), jnp.int32),
            pltpu.SMEM((blocks,), jnp.int32),
            pltpu.SMEM((comps * comps, blocks), jnp.float32),
            pltpu.VMEM((channels, points), jnp.bfloat16),
            pltpu.VMEM(v_factor.shape, jnp.bfloat16),
            pltpu.VMEM((owned * channels, cluster), jnp.bfloat16),
            pltpu.SMEM((slot_count,), jnp.int32),
            pltpu.SMEM((groups,), jnp.int32),
            pltpu.SemaphoreType.DMA((4 + comps * comps,)),
            pltpu.SemaphoreType.DMA,
        ],
        compiler_params=pltpu.CompilerParams(vmem_limit_bytes=48 << 20),
        name="source",
    )(
        kept(dest_group[:, 0]),
        kept(src_local),
        kept(ranks),
        kept(mixing.transpose(1, 2, 0)),
        x,
        kept(v_factor),
    )
    incoming = lax.all_to_all(outgoing, "tgt", split_axis=0, concat_axis=0, tiled=True)

    def place(w):
        c, j = w // shards, w % shards
        core = lax.rem(lax.axis_index("src"), cores)
        return (j // cores) * pairing + c, (j % cores) == core

    steps = 8
    senders = groups // steps
    half = jax.ShapeDtypeStruct((chips, channels, cluster), jnp.float32)
    whole = pl.BlockSpec(half.shape, lambda i: (0, 0, 0))
    mine, other = pl.pallas_call(
        functools.partial(target_kernel, comps, place),
        grid=(steps,),
        out_shape=[half, half],
        in_specs=[hbm] * 6
        + [
            pl.BlockSpec((senders * capacity, rank_width, cluster), lambda i: (i, 0, 0)),
            pl.BlockSpec((senders, channels, capacity * rank_width), lambda i: (i, 0, 0)),
        ],
        out_specs=[whole, whole],
        scratch_shapes=[
            pltpu.SMEM((slot_count,), jnp.int32),
            pltpu.SMEM((near_count,), jnp.int32),
            pltpu.SMEM((near_count,), jnp.int32),
            pltpu.VMEM((comps, near_count, comps), jnp.float32),
            pltpu.VMEM((channels, points), jnp.bfloat16),
            pltpu.VMEM(near_matrix.shape, jnp.bfloat16),
            pltpu.VMEM((2 * chips, channels, cluster), jnp.float32),
            pltpu.SemaphoreType.DMA((6,)),
        ],
        compiler_params=pltpu.CompilerParams(vmem_limit_bytes=48 << 20),
        name="target",
    )(
        kept(slot_cluster),
        kept(near_src),
        kept(near_tgt),
        kept(near_mixing.transpose(1, 0, 2)),
        x,
        kept(near_matrix),
        kept(u_factor),
        incoming,
    )
    swapped = lax.ppermute(other, "src", [(j, j ^ 1) for j in range(shards)])
    sums = mine + swapped
    lines = [
        [c * shards + h * cores + k for h in range(shards // cores) for c in range(pairing)]
        for k in range(cores)
    ]
    parts = lax.all_to_all(
        sums.astype(jnp.bfloat16),
        ("comp", "src"),
        split_axis=0,
        concat_axis=0,
        tiled=True,
        axis_index_groups=lines,
    )
    row = (lax.axis_index("src") // cores) * pairing + lax.axis_index("comp")
    own = (jnp.arange(chips, dtype=jnp.int32) == row)[:, None, None]
    result = jnp.where(own, sums, parts.astype(jnp.float32)).sum(axis=0)
    return result.reshape(comps, vectors, cluster)


def solution(mesh):
    every = ("comp", "tgt", "src")
    placed = (
        P(None, None, ("tgt", "src")),
        P(every, None),
        P(every),
        P(every),
        P(every, None, None),
        P(every, None, None),
        P(every, None, None),
        P(every),
        P(every),
        P(every),
        P(every, None, None),
        P(every, None, None),
    )
    return jax.shard_map(
        body,
        mesh=mesh,
        in_specs=placed,
        out_specs=P(None, None, every),
        check_vma=False,
    )
```

time: 147 us -> 95.1 us (0.65)
  Pallas kernels: 61 us -> 19.7 us
  waiting for transfers between devices: 47.3 us -> 17.1 us
  blocking collectives: 22.1 us -> 46 us
  local copies, waits for them, and re-layouts: 4.81 us -> 0 us
    pallas_call x1, Pallas kernels: 47.6 us -> 10.2 us  [body(): pl.pallas_call(functools.partial(target_kernel, comps, place), grid=(step...]
    all_to_all x1, waiting for transfers between devices: 45.4 us -> 15.1 us  [body(): lax.all_to_all(sums.astype(jnp.bfloat16), ('comp', 'src'), split_axis=0,...]
    all_to_all x1, blocking collectives: 22.1 us -> 46 us  [body(): lax.all_to_all(outgoing, 'tgt', split_axis=0, concat_axis=0, tiled=True)]
    pallas_call x1, Pallas kernels: 13.4 us -> 9.45 us  [body(): pl.pallas_call(functools.partial(source_kernel, comps), grid=(groups // p...]
    unnamed x20 -> x0, local copies, waits for them, and re-layouts: 3.92 us -> none
where the time goes in v2:
time: 95.1 us; the launch traced here: 94.7 us
  blocking collectives  46 us (48%)
  Pallas kernels  19.7 us (21%)
  waiting for transfers between devices  17.1 us (18%)
  starting transfers between devices  10.3 us (11%)
  other arithmetic  1.7 us (2%)
    all_to_all x1, blocking collectives, body(): lax.all_to_all(outgoing, 'tgt', split_axis=0, concat_axis=0, tiled=True)  46 us
    all_to_all x1, waiting for transfers between devices, body(): lax.all_to_all(sums.astype(jnp.bfloat16), ('comp', 'src'), split_axis=0,...  15.1 us
    pallas_call x1, Pallas kernels, body(): pl.pallas_call(functools.partial(target_kernel, comps, place), grid=(step...  10.2 us
    pallas_call x1, Pallas kernels, body(): pl.pallas_call(functools.partial(source_kernel, comps), grid=(groups // p...  9.45 us
    all_to_all x1, starting transfers between devices, body(): lax.all_to_all(sums.astype(jnp.bfloat16), ('comp', 'src'), split_axis=0,...  8.19 us
    ppermute x1, starting transfers between devices, body(): swapped = lax.ppermute(other, 'src', [(j, j ^ 1) for j in range(shards)])  2.08 us
    ppermute x1, waiting for transfers between devices, body(): swapped = lax.ppermute(other, 'src', [(j, j ^ 1) for j in range(shards)])  1.91 us
  transfers between devices with their start and end apart: 2, of which 2 were waited for; matrix products, arithmetic and copies ran while one was open for 0% of the time, Pallas kernels for 0%

profile of v2, /device:TPU:1, one launch (start us, length us, event | category | flops | bytes accessed | tf_op | source)
XLA Modules:
  0.0 94.7 jit_solution(6198400575769359952)
XLA Ops:
  0.0 9.5 %source.1 = bf16[16,96,1024]{2,1,0:T(8,128)(2,1)S(1)} custom-call(s32[128]{0:T(128)} %bitcast.9, s32[128]{0:T(128)} %src_hbm.1, s32[128]{0:T(128)} %ranks_hbm.1, f32[3,3,128]{2,1,0:T(4,128)} %bitcast.7, bf16[96,512]{1,0:T(8,128)(2,1)} %bitcast.5, bf16[128,64,256]{2,1,0:T(8,128)(2,1)} %v_hbm.1), custom_call_target="tpu_custom_call" | custom-call | tf_op jit(solution)/shard_map/source/pallas_call | solution.py:249
  9.5 46.0 %all_to_all.10.sent = bf16[16,96,1024]{2,1,0:T(8,128)(2,1)S(1)} all-to-all(bf16[16,96,1024]{2,1,0:T(8,128)(2,1)S(1)} %source.1), channel_id=1, replica_groups=mesh['comp'=2,'tgt'=16,'src'=8] {'tgt'}, dimensions={0} | all-to-all | bytes 6291456 | tf_op jit(solution)/shard_map/all_to_all | solution.py:278
  55.4 10.2 %target.1 = (f32[8,96,256]{2,1,0:T(8,128)S(1)}, f32[8,96,256]{2,1,0:T(8,128)S(1)}) custom-call(s32[256]{0:T(256)} %clusters_hbm.1, s32[4]{0:T(128)} %near_src_hbm.1, s32[4]{0:T(128)} %near_tgt_hbm.1, f32[3,4,3]{2,1,0:T(4,128)} %bitcast.8, bf16[96,512]{1,0:T(8,128)(2,1)} %bitcast.6, bf16[4,256,256]{2,1,0:T(8,128)(2,1)} %near_hbm.1, bf16[256,64,256]{2,1,0:T(8,128)(2,1)} %u.1, ...), custom_call_target="tpu_custom_call" | custom-call | tf_op jit(solution)/shard_map/target/pallas_call | solution.py:289
  65.7 2.1 %collective-permute-start = (f32[8,96,256]{2,1,0:T(8,128)S(1)}, f32[8,96,256]{2,1,0:T(8,128)S(1)}, u32[]{:S(2)}, u32[]{:S(2)}) collective-permute-start(f32[8,96,256]{2,1,0:T(8,128)S(1)} %get-tuple-element.8), channel_id=1, source_target_pairs={{0,1},{1,0},{2,3},{3,2},{4,5},{5,4},{6,7},{7,6},{8,9},{9,8},{10,11... | collective-permute-start | bytes 2359304 | tf_op jit(solution)/shard_map/ppermute | solution.py:321
  67.8 1.9 %collective-permute-done = f32[8,96,256]{2,1,0:T(8,128)S(1)} collective-permute-done((f32[8,96,256]{2,1,0:T(8,128)S(1)}, f32[8,96,256]{2,1,0:T(8,128)S(1)}, u32[]{:S(2)}, u32[]{:S(2)}) %collective-permute-start) | collective-permute-done | bytes 786464 | tf_op jit(solution)/shard_map/ppermute | solution.py:321
  69.7 0.9 fusion
  70.6 8.2 %all-to-all-start.1 = ((bf16[8,96,256]{2,1,0:T(8,128)(2,1)}), bf16[8,96,256]{2,1,0:T(8,128)(2,1)S(1)}, u32[]{:S(2)}, u32[]{:S(2)}) async-start(bf16[8,96,256]{2,1,0:T(8,128)(2,1)} %get-tuple-element.9), calls=%async_computation.1 | async-start | bytes 786432 | tf_op jit(solution)/shard_map/all_to_all | solution.py:327
  78.8 15.1 %all-to-all-done.1 = bf16[8,96,256]{2,1,0:T(8,128)(2,1)S(1)} async-done(((bf16[8,96,256]{2,1,0:T(8,128)(2,1)}), bf16[8,96,256]{2,1,0:T(8,128)(2,1)S(1)}, u32[]{:S(2)}, u32[]{:S(2)}) %all-to-all-start.1) | async-done | bytes 393248 | tf_op jit(solution)/shard_map/all_to_all | solution.py:327
  93.9 0.8 select_reduce_fusion
  (1 shorter events, 0.0 us)
Async XLA Ops:
  65.7 4.0 %collective-permute-start = (f32[8,96,256]{2,1,0:T(8,128)S(1)}, f32[8,96,256]{2,1,0:T(8,128)S(1)}, u32[]{:S(2)}, u32[]{:S(2)}) collective-permute-start(f32[8,96,256]{2,1,0:T(8,128)S(1)} %get-tuple-element.8), channel_id=1, source_target_pairs={{0,1},{1,0},{2,3},{3,2},{4,5},{5,4},{6,7},{7,6},{8,9},{9,8},{10,11... | collective-permute-start | bytes 2359304 | tf_op jit(solution)/shard_map/ppermute | solution.py:321
  70.6 23.3 %all-to-all-start.1 = ((bf16[8,96,256]{2,1,0:T(8,128)(2,1)}), bf16[8,96,256]{2,1,0:T(8,128)(2,1)S(1)}, u32[]{:S(2)}, u32[]{:S(2)}) async-start(bf16[8,96,256]{2,1,0:T(8,128)(2,1)} %get-tuple-element.9), calls=%async_computation.1 | async-start | bytes 786432 | tf_op jit(solution)/shard_map/all_to_all | solution.py:327

commit v3 on v0

v3 whole, which is shorter than its diff:
```python
import functools

import jax
import jax.numpy as jnp
from jax import lax
from jax.experimental import pallas as pl
from jax.experimental.pallas import tpu as pltpu
from jax.sharding import PartitionSpec as P

SUB = 8
QUAD = 4
TOGETHER = 8
PIECES = 4
UNROLL = 4
SOURCE_MIB = 20
TARGET_MIB = 20


def pieces(length):
    size = length // PIECES
    return [pl.ds(n * size, size) for n in range(PIECES)]


def spread(values, lane, width):
    out = values[-1]
    for t in range(len(values) - 2, -1, -1):
        out = jnp.where(lane < (t + 1) * width, values[t], out)
    return out


def source_kernel(
    comps,
    place,
    dest_hbm,
    src_hbm,
    ranks_hbm,
    mixing_hbm,
    near_src_hbm,
    near_tgt_hbm,
    near_mixing_hbm,
    field_hbm,
    near_hbm,
    v_hbm,
    u_hbm,
    out,
    u,
    table,
    dest,
    src,
    ranks,
    mixing,
    near_src,
    near_tgt,
    near_mixing,
    field,
    near,
    v,
    x,
    slots,
    sets,
    counts,
    small_sems,
    big_sems,
):
    blocks, rank_width, cluster = v.shape
    groups, channels, lanes = out.shape
    rhs = channels // comps
    owned = x.shape[0] // channels
    capacity = slots.shape[0] // groups
    near_count = near.shape[0]

    pairs = [
        (dest_hbm, dest),
        (src_hbm, src),
        (ranks_hbm, ranks),
        (near_src_hbm, near_src),
        (near_tgt_hbm, near_tgt),
        (near_mixing_hbm, near_mixing),
        (field_hbm, field),
    ] + [
        (mixing_hbm.at[e, e2], mixing.at[e * comps + e2]) for e in range(comps) for e2 in range(comps)
    ]
    small = [pltpu.make_async_copy(p, q, small_sems.at[n]) for n, (p, q) in enumerate(pairs)]
    big = [
        pltpu.make_async_copy(p, q, big_sems.at[n])
        for n, (p, q) in enumerate(
            [(near_hbm, near)]
            + [(v_hbm.at[piece], v.at[piece]) for piece in pieces(blocks)]
            + [(u_hbm.at[piece], u.at[piece]) for piece in pieces(slots.shape[0])]
        )
    ]
    for copy in small + big[: 1 + PIECES]:
        copy.start()
    table[...] = jnp.zeros_like(table)
    out[...] = jnp.zeros_like(out)
    for g in range(groups):
        counts[g] = 0
    for copy in small:
        copy.wait()

    def put(b, carry):
        g = dest[b]
        k = counts[g]
        counts[g] = k + 1
        slots[g * capacity + k] = b
        return carry

    lax.fori_loop(0, blocks, put, 0, unroll=8)
    used = jnp.int32(0)
    for g in range(groups):
        for q in range(capacity // QUAD):
            sets[used] = g * (capacity // QUAD) + q
            used = used + (counts[g] > q * QUAD).astype(jnp.int32)
    for n in range(TOGETHER):
        sets[used + n] = sets[0]
    for s in range(owned):
        x[s * channels : (s + 1) * channels, :] = field[:, s * cluster : (s + 1) * cluster]
    big[0].wait()
    for n in range(near_count):
        begin = pl.multiple_of(near_src[n] * channels, channels)
        y = lax.dot_general(
            x[pl.ds(begin, channels), :],
            near[n],
            (((1,), (1,)), ((), ())),
            preferred_element_type=jnp.float32,
        )
        parts = [y[e * rhs : (e + 1) * rhs] for e in range(comps)]
        row = place(near_tgt[n])
        for e in range(comps):
            total = None
            for e2 in range(comps):
                term = near_mixing[e, n : n + 1, e2 : e2 + 1] * parts[e2]
                total = term if total is None else total + term
            table[row, e * rhs : (e + 1) * rhs, :] += total
    for copy in big[1 : 1 + PIECES]:
        copy.wait()
    for copy in big[1 + PIECES :]:
        copy.start()

    width = QUAD * rank_width
    lane = lax.broadcasted_iota(jnp.int32, (SUB, width), 1)
    within = lane & (rank_width - 1)

    def one_set(number):
        g = lax.div(number, capacity // QUAD)
        begin = lax.rem(number, capacity // QUAD) * QUAD
        count = counts[g]
        first = number * QUAD
        full = [count > begin + t for t in range(QUAD)]
        ids = [jnp.where(full[t], slots[first + t], 0) for t in range(QUAD)]
        basis = jnp.concatenate([v[b] for b in ids], axis=0)
        y = lax.dot_general(
            x[...], basis, (((1,), (1,)), ((), ())), preferred_element_type=jnp.float32
        ).reshape(owned, comps, rhs // SUB, SUB, width)
        which = spread([src[b] for b in ids], lane, rank_width)
        picked = y[0]
        for s in range(1, owned):
            picked = jnp.where(which == s, y[s], picked)
        limit = spread(
            [jnp.where(full[t], ranks[ids[t]], 0) for t in range(QUAD)], lane, rank_width
        )
        kept = within < limit
        cols = pl.ds(pl.multiple_of(begin * rank_width, width), width)
        for e in range(comps):
            total = None
            for e2 in range(comps):
                m = spread([mixing[e * comps + e2, b] for b in ids], lane, rank_width)
                m = jnp.where(kept, m, 0.0)
                term = m * picked[e2]
                total = term if total is None else total + term
            out[g, e * rhs : (e + 1) * rhs, cols] = total.reshape(rhs, width).astype(out.dtype)

    def one_pass(n, carry):
        for m in range(TOGETHER):
            one_set(sets[n * TOGETHER + m])
        return carry

    lax.fori_loop(0, lax.div(used + TOGETHER - 1, TOGETHER), one_pass, 0)
    for copy in big[1 + PIECES :]:
        copy.wait()


def target_kernel(place, clusters_hbm, u, sent, near_table, table, other, clusters, sem):
    senders, channels, lanes = sent.shape
    slot_count, rank_width, cluster = u.shape
    capacity = slot_count // senders
    width = QUAD * rank_width
    copy = pltpu.make_async_copy(clusters_hbm, clusters, sem)
    copy.start()
    lane = lax.broadcasted_iota(jnp.int32, (1, width), 1)
    inside = [(lane >= t * rank_width) & (lane < (t + 1) * rank_width) for t in range(QUAD)]
    copy.wait()

    def one_sender(i, carry):
        for q in range(capacity // QUAD):
            a = sent[i, :, q * width : (q + 1) * width]
            first = i * capacity + q * QUAD
            basis = u[pl.ds(first, QUAD)].reshape(width, cluster)
            one = jnp.concatenate([jnp.where(m, a, jnp.zeros_like(a)) for m in inside], axis=0)
            far = jnp.dot(one, basis, preferred_element_type=jnp.float32)
            for t in range(QUAD):
                row = place(clusters[first + t])
                table[row] += far[t * channels : (t + 1) * channels]
        return carry

    lax.fori_loop(0, senders, one_sender, 0, unroll=UNROLL)
    other[...] = table[other.shape[0] :]


def body(
    field,
    dest_group,
    src_local,
    ranks,
    mixing,
    v_factor,
    u_factor,
    slot_cluster,
    near_src,
    near_tgt,
    near_mixing,
    near_matrix,
):
    groups = lax.axis_size("tgt")
    shards = lax.axis_size("src")
    pairing = lax.axis_size("comp")
    blocks, rank_width, cluster = v_factor.shape
    comps, vectors, points = field.shape
    channels = comps * vectors
    owned = points // cluster
    slot_count = u_factor.shape[0]
    capacity = slot_count // groups
    near_count = near_matrix.shape[0]
    cores = 2
    chips = pairing * shards // cores
    kept = functools.partial(pltpu.with_memory_space_constraint, memory_space=pltpu.HBM)
    hbm = pl.BlockSpec(memory_space=pltpu.HBM)

    x = kept(field.reshape(channels, points))
    def place(w):
        c, j = lax.div(w, shards), lax.rem(w, shards)
        same = lax.rem(j, cores) == lax.rem(lax.axis_index("src"), cores)
        return lax.div(j, cores) * pairing + c + jnp.where(same, 0, chips)

    vmem = pl.BlockSpec(memory_space=pltpu.VMEM)
    table_shape = (cores * chips, channels, cluster)
    outgoing, u_near, near_table = pl.pallas_call(
        functools.partial(source_kernel, comps, place),
        out_shape=[
            jax.ShapeDtypeStruct((groups, channels, capacity * rank_width), jnp.bfloat16),
            jax.ShapeDtypeStruct(u_factor.shape, jnp.bfloat16),
            jax.ShapeDtypeStruct(table_shape, jnp.float32),
        ],
        in_specs=[hbm] * 11,
        out_specs=[vmem] * 3,
        scratch_shapes=[
            pltpu.SMEM((blocks,), jnp.int32),
            pltpu.SMEM((blocks,), jnp.int32),
            pltpu.SMEM((blocks,), jnp.int32),
            pltpu.SMEM((comps * comps, blocks), jnp.float32),
            pltpu.SMEM((near_count,), jnp.int32),
            pltpu.SMEM((near_count,), jnp.int32),
            pltpu.VMEM((comps, near_count, comps), jnp.float32),
            pltpu.VMEM((channels, points), jnp.bfloat16),
            pltpu.VMEM(near_matrix.shape, jnp.bfloat16),
            pltpu.VMEM(v_factor.shape, jnp.bfloat16),
            pltpu.VMEM((owned * channels, cluster), jnp.bfloat16),
            pltpu.SMEM((slot_count,), jnp.int32),
            pltpu.SMEM((slot_count // QUAD + TOGETHER,), jnp.int32),
            pltpu.SMEM((groups,), jnp.int32),
            pltpu.SemaphoreType.DMA((7 + comps * comps,)),
            pltpu.SemaphoreType.DMA((1 + 2 * PIECES,)),
        ],
        compiler_params=pltpu.CompilerParams(vmem_limit_bytes=SOURCE_MIB << 20),
        name="source",
    )(
        kept(dest_group[:, 0]),
        kept(src_local),
        kept(ranks),
        kept(mixing.transpose(1, 2, 0)),
        kept(near_src),
        kept(near_tgt),
        kept(near_mixing.transpose(1, 0, 2)),
        x,
        kept(near_matrix),
        kept(v_factor),
        kept(u_factor),
    )
    incoming = lax.all_to_all(outgoing, "tgt", split_axis=0, concat_axis=0, tiled=True)
    table, other = pl.pallas_call(
        functools.partial(target_kernel, place),
        out_shape=[
            jax.ShapeDtypeStruct(table_shape, jnp.float32),
            jax.ShapeDtypeStruct((chips, channels, cluster), jnp.float32),
        ],
        in_specs=[hbm] + [vmem] * 3,
        out_specs=[vmem] * 2,
        scratch_shapes=[pltpu.SMEM((slot_count,), jnp.int32), pltpu.SemaphoreType.DMA],
        input_output_aliases={3: 0},
        compiler_params=pltpu.CompilerParams(vmem_limit_bytes=TARGET_MIB << 20),
        name="target",
    )(kept(slot_cluster), u_near, incoming, near_table)
    mine = table[:chips]
    swapped = lax.ppermute(other, "src", [(j, j ^ 1) for j in range(shards)])
    sums = mine + swapped
    lines = [
        [c * shards + h * cores + k for h in range(shards // cores) for c in range(pairing)]
        for k in range(cores)
    ]
    row = lax.div(lax.axis_index("src"), cores) * pairing + lax.axis_index("comp")
    own = (jnp.arange(chips, dtype=jnp.int32) == row)[:, None, None]
    sending, own = lax.optimization_barrier((sums.astype(jnp.bfloat16), own))
    parts = lax.all_to_all(
        sending, ("comp", "src"), split_axis=0, concat_axis=0, tiled=True, axis_index_groups=lines
    )
    result = jnp.where(own, sums, parts.astype(jnp.float32)).sum(axis=0)
    return result.reshape(comps, vectors, cluster)


def solution(mesh):
    every = ("comp", "tgt", "src")
    placed = (
        P(None, None, ("tgt", "src")),
        P(every, None),
        P(every),
        P(every),
        P(every, None, None),
        P(every, None, None),
        P(every, None, None),
        P(every),
        P(every),
        P(every),
        P(every, None, None),
        P(every, None, None),
    )
    return jax.shard_map(
        body,
        mesh=mesh,
        in_specs=placed,
        out_specs=P(None, None, every),
        check_vma=False,
    )
```

time: 212 us -> 84.4 us (0.40)
  matrix products: 73.5 us -> 0 us
  waiting for transfers between devices: 44.8 us -> 1.91 us
  local copies, waits for them, and re-layouts: 30.7 us -> 0 us
  blocking collectives: 49.9 us -> 67.8 us
  Pallas kernels: 0 us -> 11.4 us
  starting transfers between devices: 7.63 us -> 2.07 us
  other arithmetic: 4.08 us -> 1.01 us
    dot_general x10 -> x0, matrix products: 73.5 us -> none  [the longest x1 21.3 us: body(): far_part = jnp.einsum('st,sfq->ftq', far_spread, contrib, precision=highest)]
    all_to_all x1 -> x0, waiting for transfers between devices: 44.8 us -> none  [body(): lax.all_to_all(outgoing, 'tgt', split_axis=0, concat_axis=0, tiled=True)]
    reshape x3 -> x0, local copies, waits for them, and re-layouts: 18.3 us -> none  [the longest x1 9.63 us: body(): received = incoming.reshape(slot_count, channels, rank_width)]
    all_to_all x1 -> x2, blocking collectives: 49.9 us -> 67.8 us  [the longest x1 46 us: body(): lax.all_to_all(outgoing, 'tgt', split_axis=0, concat_axis=0, tiled=True)]
    pallas_call x0 -> x2, Pallas kernels: none -> 11.4 us  [the longest x1 6.1 us: body(): pl.pallas_call(functools.partial(source_kernel, comps, place), out_shape=...]
    all_to_all x1 -> x0, starting transfers between devices: 7.63 us -> none  [body(): lax.all_to_all(outgoing, 'tgt', split_axis=0, concat_axis=0, tiled=True)]
    convert_element_type x1 -> x0, local copies, waits for them, and re-layouts: 5.95 us -> none  [body(): mixed_coef.reshape(blocks, channels * rank_width).astype(jnp.bfloat16)]
    mul x1 -> x0, local copies, waits for them, and re-layouts: 5.34 us -> none  [body(): coefficients * rank_mask[:, None, :]]
  transfers between devices with their start and end apart: 1 -> 1, of which waited for: 1 -> 1; matrix products, arithmetic and copies ran while one was open for 1% -> 0% of each run, Pallas kernels for 0% -> 0%
where the time goes in v3:
time: 84.4 us; the launch traced here: 84.2 us
  blocking collectives  67.8 us (80%)
  Pallas kernels  11.4 us (14%)
  starting transfers between devices  2.07 us (2%)
  waiting for transfers between devices  1.91 us (2%)
  other arithmetic  1.01 us (1%)
    all_to_all x1, blocking collectives, body(): lax.all_to_all(outgoing, 'tgt', split_axis=0, concat_axis=0, tiled=True)  46 us
    all_to_all x1, blocking collectives, body(): lax.all_to_all(sending, ('comp', 'src'), split_axis=0, concat_axis=0, til...  21.9 us
    pallas_call x1, Pallas kernels, body(): pl.pallas_call(functools.partial(source_kernel, comps, place), out_shape=...  6.1 us
    pallas_call x1, Pallas kernels, body(): pl.pallas_call(functools.partial(target_kernel, place), out_shape=[jax.Sh...  5.3 us
    ppermute x1, starting transfers between devices, body(): swapped = lax.ppermute(other, 'src', [(j, j ^ 1) for j in range(shards)])  2.07 us
    ppermute x1, waiting for transfers between devices, body(): swapped = lax.ppermute(other, 'src', [(j, j ^ 1) for j in range(shards)])  1.91 us
  transfers between devices with their start and end apart: 1, of which 1 were waited for; matrix products, arithmetic and copies ran while one was open for 0% of the time, Pallas kernels for 0%

profile of v3, /device:TPU:1, one launch (start us, length us, event | category | flops | bytes accessed | tf_op | source)
XLA Modules:
  0.0 84.2 jit_solution(17785512769010547581)
XLA Ops:
  0.0 6.1 %source.1 = (bf16[16,96,1024]{2,1,0:T(8,128)(2,1)S(1)}, bf16[256,64,256]{2,1,0:T(8,128)(2,1)S(1)}, f32[16,96,256]{2,1,0:T(8,128)S(1)}) custom-call(s32[128]{0:T(128)} %bitcast.9, s32[128]{0:T(128)} %src_hbm.1, s32[128]{0:T(128)} %ranks_hbm.1, f32[3,3,128]{2,1,0:T(4,128)} %bitcast.7, s32[4]{0:T(128)} %near_src_hbm.1, s32[4]{0:T(128)} %near_tgt_hbm.1, ...), custom_call_target="tpu_custom_call" | custom-call | tf_op jit(solution)/shard_map/source/pallas_call | solution.py:247
  6.1 46.0 %all_to_all.10.sent = bf16[16,96,1024]{2,1,0:T(8,128)(2,1)S(1)} all-to-all(bf16[16,96,1024]{2,1,0:T(8,128)(2,1)S(1)} %get-tuple-element.13), channel_id=1, replica_groups=mesh['comp'=2,'tgt'=16,'src'=8] {'tgt'}, dimensions={0} | all-to-all | bytes 6291456 | tf_op jit(solution)/shard_map/all_to_all | solution.py:289
  52.1 5.3 %target.1 = (f32[16,96,256]{2,1,0:T(8,128)S(1)}, f32[8,96,256]{2,1,0:T(8,128)S(1)}) custom-call(s32[256]{0:T(256)} %clusters_hbm.1, bf16[256,64,256]{2,1,0:T(8,128)(2,1)S(1)} %get-tuple-element.12.u, bf16[16,96,1024]{2,1,0:T(8,128)(2,1)S(1)} %all_to_all.10.sent, f32[16,96,256]{2,1,0:T(8,128)S(1)} %get-tuple-element.14.near_table), custom_call_target="tpu_custom_call", output_to_operand_aliasing={{0}: (3, {})} | custom-call | tf_op jit(solution)/shard_map/target/pallas_call | solution.py:290
  57.4 2.1 %collective-permute-start = (f32[8,96,256]{2,1,0:T(8,128)S(1)}, f32[8,96,256]{2,1,0:T(8,128)S(1)}, u32[]{:S(2)}, u32[]{:S(2)}) collective-permute-start(f32[8,96,256]{2,1,0:T(8,128)S(1)} %get-tuple-element.16), channel_id=1, source_target_pairs={{0,1},{1,0},{2,3},{3,2},{4,5},{5,4},{6,7},{7,6},{8,9},{9,8},{10,11... | collective-permute-start | bytes 2359304 | tf_op jit(solution)/shard_map/ppermute | solution.py:304
  59.5 1.9 %collective-permute-done = f32[8,96,256]{2,1,0:T(8,128)S(1)} collective-permute-done((f32[8,96,256]{2,1,0:T(8,128)S(1)}, f32[8,96,256]{2,1,0:T(8,128)S(1)}, u32[]{:S(2)}, u32[]{:S(2)}) %collective-permute-start) | collective-permute-done | bytes 786464 | tf_op jit(solution)/shard_map/ppermute | solution.py:304
  61.4 0.1 fusion
  61.5 21.9 %all_to_all.11 = bf16[8,96,256]{2,1,0:T(8,128)(2,1)S(1)} all-to-all(bf16[8,96,256]{2,1,0:T(8,128)(2,1)S(1)} %fusion), channel_id=1, replica_groups={{0,128,2,130,4,132,6,134},{1,129,3,131,5,133,7,135},{8,136,10,138,12,14..., dimensions={0} | all-to-all | bytes 786432 | tf_op jit(solution)/shard_map/all_to_all | solution.py:313
  83.4 0.9 %select_reduce_fusion = f32[96,256]{1,0:T(8,128)} fusion(bf16[8,96,256]{2,1,0:T(8,128)(2,1)S(1)} %all_to_all.11, pred[8]{0:T(512)(128)(4,1)S(1)} %bitcast.10, f32[8,96,256]{2,1,0:T(8,128)S(1)} %collective-permute-done, f32[16,96,256]{2,1,0:T(8,128)S(1)} %get-tuple-element.15), kind=kLoop, calls=%fused_computation | loop fusion | flops 761856 | bytes 2064392 | tf_op jit(solution)/shard_map/reduce_sum | solution.py:316
  (1 shorter events, 0.0 us)
Async XLA Ops:
  57.4 4.0 %collective-permute-start = (f32[8,96,256]{2,1,0:T(8,128)S(1)}, f32[8,96,256]{2,1,0:T(8,128)S(1)}, u32[]{:S(2)}, u32[]{:S(2)}) collective-permute-start(f32[8,96,256]{2,1,0:T(8,128)S(1)} %get-tuple-element.16), channel_id=1, source_target_pairs={{0,1},{1,0},{2,3},{3,2},{4,5},{5,4},{6,7},{7,6},{8,9},{9,8},{10,11... | collective-permute-start | bytes 2359304 | tf_op jit(solution)/shard_map/ppermute | solution.py:304

commit v4 on v3

--- a/solution.py
+++ b/solution.py
@@ -8,10 +8,11 @@
 from jax.sharding import PartitionSpec as P
 
 SUB = 8
+LANES = 128
 QUAD = 4
 TOGETHER = 8
 PIECES = 4
-UNROLL = 4
+UNROLL = 8
 SOURCE_MIB = 20
 TARGET_MIB = 20
 
@@ -21,11 +22,10 @@
     return [pl.ds(n * size, size) for n in range(PIECES)]
 
 
-def spread(values, lane, width):
-    out = values[-1]
-    for t in range(len(values) - 2, -1, -1):
-        out = jnp.where(lane < (t + 1) * width, values[t], out)
-    return out
+def spread(values, low):
+    return jnp.concatenate(
+        [jnp.where(low, values[t], values[t + 1]) for t in range(0, len(values), 2)], axis=-1
+    )
 
 
 def source_kernel(
@@ -138,8 +138,8 @@
         copy.start()
 
     width = QUAD * rank_width
-    lane = lax.broadcasted_iota(jnp.int32, (SUB, width), 1)
-    within = lane & (rank_width - 1)
+    low = lax.broadcasted_iota(jnp.int32, (SUB, LANES), 1) < rank_width
+    within = lax.broadcasted_iota(jnp.int32, (SUB, width), 1) & (rank_width - 1)
 
     def one_set(number):
         g = lax.div(number, capacity // QUAD)
@@ -152,19 +152,17 @@
         y = lax.dot_general(
             x[...], basis, (((1,), (1,)), ((), ())), preferred_element_type=jnp.float32
         ).reshape(owned, comps, rhs // SUB, SUB, width)
-        which = spread([src[b] for b in ids], lane, rank_width)
+        which = spread([src[b] for b in ids], low)
         picked = y[0]
         for s in range(1, owned):
             picked = jnp.where(which == s, y[s], picked)
-        limit = spread(
-            [jnp.where(full[t], ranks[ids[t]], 0) for t in range(QUAD)], lane, rank_width
-        )
+        limit = spread([jnp.where(full[t], ranks[ids[t]], 0) for t in range(QUAD)], low)
         kept = within < limit
         cols = pl.ds(pl.multiple_of(begin * rank_width, width), width)
         for e in range(comps):
             total = None
             for e2 in range(comps):
-                m = spread([mixing[e * comps + e2, b] for b in ids], lane, rank_width)
+                m = spread([mixing[e * comps + e2, b] for b in ids], low)
                 m = jnp.where(kept, m, 0.0)
                 term = m * picked[e2]
                 total = term if total is None else total + term

time: 84.4 us -> 84.1 us (level)
  no operation moved by 1% of the time
where the time goes in v4:
time: 84.1 us; the launch traced here: 84 us
  blocking collectives  67.8 us (81%)
  Pallas kernels  11.1 us (13%)
  starting transfers between devices  2.07 us (2%)
  waiting for transfers between devices  1.91 us (2%)
  other arithmetic  1.01 us (1%)
    all_to_all x1, blocking collectives, body(): lax.all_to_all(outgoing, 'tgt', split_axis=0, concat_axis=0, tiled=True)  46 us
    all_to_all x1, blocking collectives, body(): lax.all_to_all(sending, ('comp', 'src'), split_axis=0, concat_axis=0, til...  21.9 us
    pallas_call x1, Pallas kernels, body(): pl.pallas_call(functools.partial(source_kernel, comps, place), out_shape=...  6.1 us
    pallas_call x1, Pallas kernels, body(): pl.pallas_call(functools.partial(target_kernel, place), out_shape=[jax.Sh...  5.02 us
    ppermute x1, starting transfers between devices, body(): swapped = lax.ppermute(other, 'src', [(j, j ^ 1) for j in range(shards)])  2.07 us
    ppermute x1, waiting for transfers between devices, body(): swapped = lax.ppermute(other, 'src', [(j, j ^ 1) for j in range(shards)])  1.91 us
  transfers between devices with their start and end apart: 1, of which 1 were waited for; matrix products, arithmetic and copies ran while one was open for 0% of the time, Pallas kernels for 0%

profile of v4, /device:TPU:1, one launch (start us, length us, event | category | flops | bytes accessed | tf_op | source)
XLA Modules:
  0.0 84.0 jit_solution(10386594557870413022)
XLA Ops:
  0.0 6.1 %source.1 = (bf16[16,96,1024]{2,1,0:T(8,128)(2,1)S(1)}, bf16[256,64,256]{2,1,0:T(8,128)(2,1)S(1)}, f32[16,96,256]{2,1,0:T(8,128)S(1)}) custom-call(s32[128]{0:T(128)} %bitcast.9, s32[128]{0:T(128)} %src_hbm.1, s32[128]{0:T(128)} %ranks_hbm.1, f32[3,3,128]{2,1,0:T(4,128)} %bitcast.7, s32[4]{0:T(128)} %near_src_hbm.1, s32[4]{0:T(128)} %near_tgt_hbm.1, ...), custom_call_target="tpu_custom_call" | custom-call | tf_op jit(solution)/shard_map/source/pallas_call | solution.py:245
  6.1 46.0 %all_to_all.10.sent = bf16[16,96,1024]{2,1,0:T(8,128)(2,1)S(1)} all-to-all(bf16[16,96,1024]{2,1,0:T(8,128)(2,1)S(1)} %get-tuple-element.13), channel_id=1, replica_groups=mesh['comp'=2,'tgt'=16,'src'=8] {'tgt'}, dimensions={0} | all-to-all | bytes 6291456 | tf_op jit(solution)/shard_map/all_to_all | solution.py:287
  52.1 5.0 %target.1 = (f32[16,96,256]{2,1,0:T(8,128)S(1)}, f32[8,96,256]{2,1,0:T(8,128)S(1)}) custom-call(s32[256]{0:T(256)} %clusters_hbm.1, bf16[256,64,256]{2,1,0:T(8,128)(2,1)S(1)} %get-tuple-element.12.u, bf16[16,96,1024]{2,1,0:T(8,128)(2,1)S(1)} %all_to_all.10.sent, f32[16,96,256]{2,1,0:T(8,128)S(1)} %get-tuple-element.14.near_table), custom_call_target="tpu_custom_call", output_to_operand_aliasing={{0}: (3, {})} | custom-call | tf_op jit(solution)/shard_map/target/pallas_call | solution.py:288
  57.1 2.1 %collective-permute-start = (f32[8,96,256]{2,1,0:T(8,128)S(1)}, f32[8,96,256]{2,1,0:T(8,128)S(1)}, u32[]{:S(2)}, u32[]{:S(2)}) collective-permute-start(f32[8,96,256]{2,1,0:T(8,128)S(1)} %get-tuple-element.16), channel_id=1, source_target_pairs={{0,1},{1,0},{2,3},{3,2},{4,5},{5,4},{6,7},{7,6},{8,9},{9,8},{10,11... | collective-permute-start | bytes 2359304 | tf_op jit(solution)/shard_map/ppermute | solution.py:302
  59.2 1.9 %collective-permute-done = f32[8,96,256]{2,1,0:T(8,128)S(1)} collective-permute-done((f32[8,96,256]{2,1,0:T(8,128)S(1)}, f32[8,96,256]{2,1,0:T(8,128)S(1)}, u32[]{:S(2)}, u32[]{:S(2)}) %collective-permute-start) | collective-permute-done | bytes 786464 | tf_op jit(solution)/shard_map/ppermute | solution.py:302
  61.1 0.1 fusion
  61.2 21.9 %all_to_all.11 = bf16[8,96,256]{2,1,0:T(8,128)(2,1)S(1)} all-to-all(bf16[8,96,256]{2,1,0:T(8,128)(2,1)S(1)} %fusion), channel_id=1, replica_groups={{0,128,2,130,4,132,6,134},{1,129,3,131,5,133,7,135},{8,136,10,138,12,14..., dimensions={0} | all-to-all | bytes 786432 | tf_op jit(solution)/shard_map/all_to_all | solution.py:311
  83.1 0.9 %select_reduce_fusion = f32[96,256]{1,0:T(8,128)} fusion(bf16[8,96,256]{2,1,0:T(8,128)(2,1)S(1)} %all_to_all.11, pred[8]{0:T(512)(128)(4,1)S(1)} %bitcast.10, f32[8,96,256]{2,1,0:T(8,128)S(1)} %collective-permute-done, f32[16,96,256]{2,1,0:T(8,128)S(1)} %get-tuple-element.15), kind=kLoop, calls=%fused_computation | loop fusion | flops 761856 | bytes 2064392 | tf_op jit(solution)/shard_map/reduce_sum | solution.py:314
  (1 shorter events, 0.0 us)
Async XLA Ops:
  57.1 4.0 %collective-permute-start = (f32[8,96,256]{2,1,0:T(8,128)S(1)}, f32[8,96,256]{2,1,0:T(8,128)S(1)}, u32[]{:S(2)}, u32[]{:S(2)}) collective-permute-start(f32[8,96,256]{2,1,0:T(8,128)S(1)} %get-tuple-element.16), channel_id=1, source_target_pairs={{0,1},{1,0},{2,3},{3,2},{4,5},{5,4},{6,7},{7,6},{8,9},{9,8},{10,11... | collective-permute-start | bytes 2359304 | tf_op jit(solution)/shard_map/ppermute | solution.py:302

commit v5 on v4

--- a/solution.py
+++ b/solution.py
@@ -205,6 +205,12 @@
     other[...] = table[other.shape[0] :]
 
 
+def combine_kernel(table, swapped, own, *sending):
+    own[...] = table[0] + swapped[0]
+    for n, part in enumerate(sending, 1):
+        part[...] = (table[n] + swapped[n]).astype(part.dtype)
+
+
 def body(
     field,
     dest_group,
@@ -237,8 +243,11 @@
     x = kept(field.reshape(channels, points))
     def place(w):
         c, j = lax.div(w, shards), lax.rem(w, shards)
-        same = lax.rem(j, cores) == lax.rem(lax.axis_index("src"), cores)
-        return lax.div(j, cores) * pairing + c + jnp.where(same, 0, chips)
+        mine = lax.axis_index("src")
+        same = lax.rem(j, cores) == lax.rem(mine, cores)
+        here = lax.div(mine, cores) * pairing + lax.axis_index("comp")
+        up = lax.div(j, cores) * pairing + c - here + chips
+        return lax.rem(up, chips) + jnp.where(same, 0, chips)
 
     vmem = pl.BlockSpec(memory_space=pltpu.VMEM)
     table_shape = (cores * chips, channels, cluster)
@@ -298,20 +307,29 @@
         compiler_params=pltpu.CompilerParams(vmem_limit_bytes=TARGET_MIB << 20),
         name="target",
     )(kept(slot_cluster), u_near, incoming, near_table)
-    mine = table[:chips]
     swapped = lax.ppermute(other, "src", [(j, j ^ 1) for j in range(shards)])
-    sums = mine + swapped
-    lines = [
-        [c * shards + h * cores + k for h in range(shards // cores) for c in range(pairing)]
-        for k in range(cores)
-    ]
-    row = lax.div(lax.axis_index("src"), cores) * pairing + lax.axis_index("comp")
-    own = (jnp.arange(chips, dtype=jnp.int32) == row)[:, None, None]
-    sending, own = lax.optimization_barrier((sums.astype(jnp.bfloat16), own))
-    parts = lax.all_to_all(
-        sending, ("comp", "src"), split_axis=0, concat_axis=0, tiled=True, axis_index_groups=lines
-    )
-    result = jnp.where(own, sums, parts.astype(jnp.float32)).sum(axis=0)
+    own, *sending = pl.pallas_call(
+        combine_kernel,
+        out_shape=[jax.ShapeDtypeStruct((channels, cluster), jnp.float32)]
+        + [jax.ShapeDtypeStruct((channels, cluster), jnp.bfloat16)] * (chips - 1),
+        in_specs=[vmem] * 2,
+        out_specs=[vmem] * chips,
+        compiler_params=pltpu.CompilerParams(vmem_limit_bytes=8 << 20),
+        name="combine",
+    )(table, swapped)
+
+    def device(z, core):
+        return (z % pairing) * shards + (z // pairing) * cores + core
+
+    result = own
+    for up in sorted(range(1, chips), key=lambda n: -min(n, chips - n)):
+        part = sending[up - 1]
+        moves = [
+            (device(z, core), device((z + up) % chips, core))
+            for z in range(chips)
+            for core in range(cores)
+        ]
+        result = result + lax.ppermute(part, ("comp", "src"), moves).astype(jnp.float32)
     return result.reshape(comps, vectors, cluster)
 
 

time: 84.1 us -> 81.7 us (0.971)
  blocking collectives: 67.8 us -> 46 us
  starting transfers between devices: 2.07 us -> 19.8 us
  waiting for transfers between devices: 1.91 us -> 3.7 us
    all_to_all x1 -> x0, blocking collectives: 21.9 us -> none  [body(): lax.all_to_all(sending, ('comp', 'src'), split_axis=0, concat_axis=0, til...]
    ppermute x0 -> x7, starting transfers between devices: none -> 17.7 us  [body(): lax.ppermute(part, ('comp', 'src'), moves).astype(jnp.float32)]
    ppermute x0 -> x7, waiting for transfers between devices: none -> 1.79 us  [body(): lax.ppermute(part, ('comp', 'src'), moves).astype(jnp.float32)]
    reduce_sum x1 -> x0, other arithmetic: 0.87 us -> none  [body(): result = jnp.where(own, sums, parts.astype(jnp.float32)).sum(axis=0)]
  transfers between devices with their start and end apart: 1 -> 8, of which waited for: 1 -> 3; matrix products, arithmetic and copies ran while one was open for 0% -> 0% of each run, Pallas kernels for 0% -> 0%
where the time goes in v5:
time: 81.7 us; the launch traced here: 81.4 us
  blocking collectives  46 us (56%)
  starting transfers between devices  19.8 us (24%)
  Pallas kernels  11.2 us (14%)
  waiting for transfers between devices  3.7 us (5%)
    all_to_all x1, blocking collectives, body(): lax.all_to_all(outgoing, 'tgt', split_axis=0, concat_axis=0, tiled=True)  46 us
    ppermute x7, starting transfers between devices, body(): lax.ppermute(part, ('comp', 'src'), moves).astype(jnp.float32)  17.7 us
    pallas_call x1, Pallas kernels, body(): pl.pallas_call(functools.partial(source_kernel, comps, place), out_shape=...  6.1 us
    pallas_call x1, Pallas kernels, body(): pl.pallas_call(functools.partial(target_kernel, place), out_shape=[jax.Sh...  5.04 us
    ppermute x1, starting transfers between devices, body(): swapped = lax.ppermute(other, 'src', [(j, j ^ 1) for j in range(shards)])  2.07 us
    ppermute x1, waiting for transfers between devices, body(): swapped = lax.ppermute(other, 'src', [(j, j ^ 1) for j in range(shards)])  1.91 us
    ppermute x7, waiting for transfers between devices, body(): lax.ppermute(part, ('comp', 'src'), moves).astype(jnp.float32)  1.79 us
  transfers between devices with their start and end apart: 8, of which 3 were waited for; matrix products, arithmetic and copies ran while one was open for 0% of the time, Pallas kernels for 0%

profile of v5, /device:TPU:1, one launch (start us, length us, event | category | flops | bytes accessed | tf_op | source)
XLA Modules:
  0.0 81.4 jit_solution(8707989584590780226)
XLA Ops:
  0.0 6.1 %source.1 = (bf16[16,96,1024]{2,1,0:T(8,128)(2,1)S(1)}, bf16[256,64,256]{2,1,0:T(8,128)(2,1)S(1)}, f32[16,96,256]{2,1,0:T(8,128)S(1)}) custom-call(s32[128]{0:T(128)} %bitcast.8, s32[128]{0:T(128)} %src_hbm.1, s32[128]{0:T(128)} %ranks_hbm.1, f32[3,3,128]{2,1,0:T(4,128)} %bitcast.6, s32[4]{0:T(128)} %near_src_hbm.1, s32[4]{0:T(128)} %near_tgt_hbm.1, ...), custom_call_target="tpu_custom_call" | custom-call | tf_op jit(solution)/shard_map/source/pallas_call | solution.py:254
  6.1 46.0 %all_to_all.5.sent = bf16[16,96,1024]{2,1,0:T(8,128)(2,1)S(1)} all-to-all(bf16[16,96,1024]{2,1,0:T(8,128)(2,1)S(1)} %get-tuple-element.19), channel_id=1, replica_groups=mesh['comp'=2,'tgt'=16,'src'=8] {'tgt'}, dimensions={0} | all-to-all | bytes 6291456 | tf_op jit(solution)/shard_map/all_to_all | solution.py:296
  52.1 5.0 %target.1 = (f32[16,96,256]{2,1,0:T(8,128)S(1)}, f32[8,96,256]{2,1,0:T(8,128)S(1)}) custom-call(s32[256]{0:T(256)} %clusters_hbm.1, bf16[256,64,256]{2,1,0:T(8,128)(2,1)S(1)} %get-tuple-element.18.u, bf16[16,96,1024]{2,1,0:T(8,128)(2,1)S(1)} %all_to_all.5.sent, f32[16,96,256]{2,1,0:T(8,128)S(1)} %get-tuple-element.20.near_table), custom_call_target="tpu_custom_call", output_to_operand_aliasing={{0}: (3, {})} | custom-call | tf_op jit(solution)/shard_map/target/pallas_call | solution.py:297
  57.1 2.1 %collective-permute-start = (f32[8,96,256]{2,1,0:T(8,128)S(1)}, f32[8,96,256]{2,1,0:T(8,128)S(1)}, u32[]{:S(2)}, u32[]{:S(2)}) collective-permute-start(f32[8,96,256]{2,1,0:T(8,128)S(1)} %get-tuple-element.22), channel_id=1, source_target_pairs={{0,1},{1,0},{2,3},{3,2},{4,5},{5,4},{6,7},{7,6},{8,9},{9,8},{10,11... | collective-permute-start | bytes 2359304 | tf_op jit(solution)/shard_map/ppermute | solution.py:310
  59.2 1.9 %collective-permute-done.swapped = f32[8,96,256]{2,1,0:T(8,128)S(1)} collective-permute-done((f32[8,96,256]{2,1,0:T(8,128)S(1)}, f32[8,96,256]{2,1,0:T(8,128)S(1)}, u32[]{:S(2)}, u32[]{:S(2)}) %collective-permute-start) | collective-permute-done | bytes 786464 | tf_op jit(solution)/shard_map/ppermute | solution.py:310
  61.1 0.1 combine.1
  61.2 7.0 %collective-permute-start.1 = (bf16[96,256]{1,0:T(8,128)(2,1)S(1)}, bf16[96,256]{1,0:T(8,128)(2,1)S(1)}, u32[]{:S(2)}, u32[]{:S(2)}) collective-permute-start(bf16[96,256]{1,0:T(8,128)(2,1)S(1)} %get-tuple-element.24), channel_id=1, source_target_pairs={{0,4},{1,5},{128,132},{129,133},{2,6},{3,7},{130,134},{131,135},{4... | collective-permute-start | bytes 147464 | tf_op jit(solution)/shard_map/ppermute | solution.py:332
  68.2 1.6 %collective-permute-start.2 = (bf16[96,256]{1,0:T(8,128)(2,1)S(1)}, bf16[96,256]{1,0:T(8,128)(2,1)S(1)}, u32[]{:S(2)}, u32[]{:S(2)}) collective-permute-start(bf16[96,256]{1,0:T(8,128)(2,1)S(1)} %get-tuple-element.25), channel_id=1, source_target_pairs={{0,130},{1,131},{128,4},{129,5},{2,132},{3,133},{130,6},{131,7},{4... | collective-permute-start | bytes 147464 | tf_op jit(solution)/shard_map/ppermute | solution.py:332
  69.8 2.8 %collective-permute-start.3 = (bf16[96,256]{1,0:T(8,128)(2,1)S(1)}, bf16[96,256]{1,0:T(8,128)(2,1)S(1)}, u32[]{:S(2)}, u32[]{:S(2)}) collective-permute-start(bf16[96,256]{1,0:T(8,128)(2,1)S(1)} %get-tuple-element.26), channel_id=1, source_target_pairs={{0,132},{1,133},{128,6},{129,7},{2,134},{3,135},{130,0},{131,1},{4... | collective-permute-start | bytes 147464 | tf_op jit(solution)/shard_map/ppermute | solution.py:332
  72.7 1.2 %collective-permute-start.4 = (bf16[96,256]{1,0:T(8,128)(2,1)S(1)}, bf16[96,256]{1,0:T(8,128)(2,1)S(1)}, u32[]{:S(2)}, u32[]{:S(2)}) collective-permute-start(bf16[96,256]{1,0:T(8,128)(2,1)S(1)} %get-tuple-element.27), channel_id=1, source_target_pairs={{0,2},{1,3},{128,130},{129,131},{2,4},{3,5},{130,132},{131,133},{4... | collective-permute-start | bytes 147464 | tf_op jit(solution)/shard_map/ppermute | solution.py:332
  73.9 2.4 %collective-permute-start.5 = (bf16[96,256]{1,0:T(8,128)(2,1)S(1)}, bf16[96,256]{1,0:T(8,128)(2,1)S(1)}, u32[]{:S(2)}, u32[]{:S(2)}) collective-permute-start(bf16[96,256]{1,0:T(8,128)(2,1)S(1)} %get-tuple-element.28), channel_id=1, source_target_pairs={{0,6},{1,7},{128,134},{129,135},{2,0},{3,1},{130,128},{131,129},{4... | collective-permute-start | bytes 147464 | tf_op jit(solution)/shard_map/ppermute | solution.py:332
  76.2 0.0 collective-permute-done.1
  76.2 0.7 collective-permute-start.6
  77.0 0.0 collective-permute-done.2
  77.0 1.9 %collective-permute-start.7 = (bf16[96,256]{1,0:T(8,128)(2,1)S(1)}, bf16[96,256]{1,0:T(8,128)(2,1)S(1)}, u32[]{:S(2)}, u32[]{:S(2)}) collective-permute-start(bf16[96,256]{1,0:T(8,128)(2,1)S(1)} %get-tuple-element.30), channel_id=1, source_target_pairs={{0,134},{1,135},{128,0},{129,1},{2,128},{3,129},{130,2},{131,3},{4... | collective-permute-start | bytes 147464 | tf_op jit(solution)/shard_map/ppermute | solution.py:332
  78.9 0.0 collective-permute-done.3
  78.9 0.0 collective-permute-done.4
  78.9 0.0 collective-permute-done.5
  78.9 1.6 %collective-permute-done.6 = bf16[96,256]{1,0:T(8,128)(2,1)S(1)} collective-permute-done((bf16[96,256]{1,0:T(8,128)(2,1)S(1)}, bf16[96,256]{1,0:T(8,128)(2,1)S(1)}, u32[]{:S(2)}, u32[]{:S(2)}) %collective-permute-start.6) | collective-permute-done | bytes 49184 | tf_op jit(solution)/shard_map/ppermute | solution.py:332
  80.5 0.2 collective-permute-done.7
  80.7 0.7 convert_add_fusion
Async XLA Ops:
  57.1 4.0 %collective-permute-start = (f32[8,96,256]{2,1,0:T(8,128)S(1)}, f32[8,96,256]{2,1,0:T(8,128)S(1)}, u32[]{:S(2)}, u32[]{:S(2)}) collective-permute-start(f32[8,96,256]{2,1,0:T(8,128)S(1)} %get-tuple-element.22), channel_id=1, source_target_pairs={{0,1},{1,0},{2,3},{3,2},{4,5},{5,4},{6,7},{7,6},{8,9},{9,8},{10,11... | collective-permute-start | bytes 2359304 | tf_op jit(solution)/shard_map/ppermute | solution.py:310
  61.2 15.1 %collective-permute-start.1 = (bf16[96,256]{1,0:T(8,128)(2,1)S(1)}, bf16[96,256]{1,0:T(8,128)(2,1)S(1)}, u32[]{:S(2)}, u32[]{:S(2)}) collective-permute-start(bf16[96,256]{1,0:T(8,128)(2,1)S(1)} %get-tuple-element.24), channel_id=1, source_target_pairs={{0,4},{1,5},{128,132},{129,133},{2,6},{3,7},{130,134},{131,135},{4... | collective-permute-start | bytes 147464 | tf_op jit(solution)/shard_map/ppermute | solution.py:332
  68.2 8.8 %collective-permute-start.2 = (bf16[96,256]{1,0:T(8,128)(2,1)S(1)}, bf16[96,256]{1,0:T(8,128)(2,1)S(1)}, u32[]{:S(2)}, u32[]{:S(2)}) collective-permute-start(bf16[96,256]{1,0:T(8,128)(2,1)S(1)} %get-tuple-element.25), channel_id=1, source_target_pairs={{0,130},{1,131},{128,4},{129,5},{2,132},{3,133},{130,6},{131,7},{4... | collective-permute-start | bytes 147464 | tf_op jit(solution)/shard_map/ppermute | solution.py:332
  69.8 9.1 %collective-permute-start.3 = (bf16[96,256]{1,0:T(8,128)(2,1)S(1)}, bf16[96,256]{1,0:T(8,128)(2,1)S(1)}, u32[]{:S(2)}, u32[]{:S(2)}) collective-permute-start(bf16[96,256]{1,0:T(8,128)(2,1)S(1)} %get-tuple-element.26), channel_id=1, source_target_pairs={{0,132},{1,133},{128,6},{129,7},{2,134},{3,135},{130,0},{131,1},{4... | collective-permute-start | bytes 147464 | tf_op jit(solution)/shard_map/ppermute | solution.py:332
  72.7 6.3 %collective-permute-start.4 = (bf16[96,256]{1,0:T(8,128)(2,1)S(1)}, bf16[96,256]{1,0:T(8,128)(2,1)S(1)}, u32[]{:S(2)}, u32[]{:S(2)}) collective-permute-start(bf16[96,256]{1,0:T(8,128)(2,1)S(1)} %get-tuple-element.27), channel_id=1, source_target_pairs={{0,2},{1,3},{128,130},{129,131},{2,4},{3,5},{130,132},{131,133},{4... | collective-permute-start | bytes 147464 | tf_op jit(solution)/shard_map/ppermute | solution.py:332
  73.9 5.1 %collective-permute-start.5 = (bf16[96,256]{1,0:T(8,128)(2,1)S(1)}, bf16[96,256]{1,0:T(8,128)(2,1)S(1)}, u32[]{:S(2)}, u32[]{:S(2)}) collective-permute-start(bf16[96,256]{1,0:T(8,128)(2,1)S(1)} %get-tuple-element.28), channel_id=1, source_target_pairs={{0,6},{1,7},{128,134},{129,135},{2,0},{3,1},{130,128},{131,129},{4... | collective-permute-start | bytes 147464 | tf_op jit(solution)/shard_map/ppermute | solution.py:332
  76.2 4.3 %collective-permute-start.6 = (bf16[96,256]{1,0:T(8,128)(2,1)S(1)}, bf16[96,256]{1,0:T(8,128)(2,1)S(1)}, u32[]{:S(2)}, u32[]{:S(2)}) collective-permute-start(bf16[96,256]{1,0:T(8,128)(2,1)S(1)} %get-tuple-element.29), channel_id=1, source_target_pairs={{0,128},{1,129},{128,2},{129,3},{2,130},{3,131},{130,4},{131,5},{4... | collective-permute-start | bytes 147464 | tf_op jit(solution)/shard_map/ppermute | solution.py:332
  77.0 3.7 %collective-permute-start.7 = (bf16[96,256]{1,0:T(8,128)(2,1)S(1)}, bf16[96,256]{1,0:T(8,128)(2,1)S(1)}, u32[]{:S(2)}, u32[]{:S(2)}) collective-permute-start(bf16[96,256]{1,0:T(8,128)(2,1)S(1)} %get-tuple-element.30), channel_id=1, source_target_pairs={{0,134},{1,135},{128,0},{129,1},{2,128},{3,129},{130,2},{131,3},{4... | collective-permute-start | bytes 147464 | tf_op jit(solution)/shard_map/ppermute | solution.py:332
